TPU v7x, 128 devices: a whole 4x4x4 slice. The times are simulated.
128 devices in a mesh: tok: 4 (over z_lo, core), con: 4 (over x), out: 8 (over z_hi, y).
Axes of the slice: x: 4, y: 4, z: 4 (z_hi: 2, z_lo: 2; z = z_hi * 2 + z_lo), core: 2. Of those that a mesh axis runs over, the one named last changes fastest.
Arguments:
- tokens: bfloat16 [1024, 10240], P('tok', 'con'), may hold values from -6 to 6
- out_grad: bfloat16 [1024, 10240], P('tok', 'con'), may hold values from -3 to 3
- weight_in: bfloat16 [10240, 20480], P('con', ('tok', 'out')), may hold values from -0.0625 to 0.0625
- weight_out: bfloat16 [20480, 10240], P(('tok', 'out'), 'con'), may hold values from -0.0390625 to 0.0390625
Outputs:
- input_grad: bfloat16 [1024, 10240], P(('tok', 'out'), 'con')
- first_grad: float32 [10240, 20480], P('con', ('tok', 'out'))
- second_grad: float32 [20480, 10240], P(('tok', 'out'), 'con')
All inputs are finite; a program needn't handle non-finite values.
Results may differ from a plain program's by a relative error of at most 0.0049.
Values may be sent and summed in bfloat16 or wider, within the bound.
No kernel may reach another device: no remote copies, remote signals or barrier semaphores. Data moves between devices by JAX's collectives and lax.ppermute only.
A program may use at most 128 MiB of HBM per device.

v0:
```python
import jax
import jax.numpy as jnp
from jax import lax
from jax.sharding import PartitionSpec as P


def gelu_parts(pre, act_grad):
    cdf = 0.5 * (1.0 + jax.scipy.special.erf(pre * 0.7071067811865476))
    density = jnp.exp(-0.5 * pre * pre) * 0.3989422804014327
    activ = (pre * cdf).astype(jnp.bfloat16)
    pre_grad = (act_grad * (cdf + pre * density)).astype(jnp.bfloat16)
    return (activ, pre_grad)


def per_device(tokens, out_grad, weight_in, weight_out):
    gathered_tok, gathered_grad = (
        lax.all_gather(tokens, "tok", axis=0, tiled=True),
        lax.all_gather(out_grad, "tok", axis=0, tiled=True),
    )
    pre_part = jnp.dot(gathered_tok, weight_in, preferred_element_type=jnp.float32)
    grad_part = lax.dot_general(
        gathered_grad, weight_out, (((1,), (1,)), ((), ())), preferred_element_type=jnp.float32
    )
    pre, act_grad = lax.psum((pre_part, grad_part), "con")
    activ, pre_grad = gelu_parts(pre, act_grad)
    first_grad = lax.dot_general(
        gathered_tok, pre_grad, (((0,), (0,)), ((), ())), preferred_element_type=jnp.float32
    )
    second_grad = lax.dot_general(
        activ, gathered_grad, (((0,), (0,)), ((), ())), preferred_element_type=jnp.float32
    )
    summed = lax.psum_scatter(
        lax.dot_general(
            pre_grad, weight_in, (((1,), (1,)), ((), ())), preferred_element_type=jnp.float32
        ),
        ("tok", "out"),
        scatter_dimension=0,
        tiled=True,
    )
    return (summed.astype(jnp.bfloat16), first_grad, second_grad)


def solution(mesh):
    placed = (P("tok", "con"), P("tok", "con"), P("con", ("tok", "out")), P(("tok", "out"), "con"))
    return jax.shard_map(
        per_device,
        mesh=mesh,
        in_specs=placed,
        out_specs=(P(("tok", "out"), "con"), P("con", ("tok", "out")), P(("tok", "out"), "con")),
        check_vma=False,
    )
```

profile of v0, /device:TPU:26, one launch (start us, length us, event | category | flops | bytes accessed | tf_op | source)
XLA Modules:
  0.0 438.6 jit_solution(11786640155277822944)
XLA Ops:
  7.2 0.0 copy-start
  7.2 0.0 all-gather.3.cloned.1.call-start
  7.2 0.7 all-gather.3.cloned.1.call-update
  7.9 0.0 all-gather.5.cloned.1.call-start
  8.0 0.7 all-gather.5.cloned.1.call-update
  8.7 0.0 all-reduce.3.cloned.1.call-start
  8.7 57.5 %all-gather.3.cloned.1.call-done = bf16[1024,2560]{1,0:T(8,128)(2,1)} async-done(((bf16[256,2560]{1,0:T(8,128)(2,1)}), bf16[1024,2560]{1,0:T(8,128)(2,1)}) %all-gather.3.cloned.1.call-update) | async-done | bytes 5242896 | tf_op jit(solution)/shard_map/all_gather | solution.py:18
  66.2 9.2 %fusion.7 = f32[1024,640]{1,0:T(8,128)} fusion(bf16[1024,2560]{1,0:T(8,128)(2,1)} %all-gather.3.cloned.1.call-done, bf16[640,2560]{1,0:T(8,128)(2,1)} %param.7), kind=kOutput, calls=%fused_computation.11 | convolution fusion | flops 3355443200 | bytes 11141120 | tf_op jit(solution)/shard_map/dot_general | solution.py:21
  75.4 48.6 %all-gather.5.cloned.1.call-done = bf16[1024,2560]{1,0:T(8,128)(2,1)} async-done(((bf16[256,2560]{1,0:T(8,128)(2,1)}), bf16[1024,2560]{1,0:T(8,128)(2,1)}) %all-gather.5.cloned.1.call-update) | async-done | bytes 5242896 | tf_op jit(solution)/shard_map/all_gather | solution.py:17
  124.0 0.0 copy-done
  124.0 8.2 %fusion.8 = f32[1024,640]{1,0:T(8,128)} fusion(bf16[1024,2560]{1,0:T(8,128)(2,1)} %all-gather.5.cloned.1.call-done, bf16[2560,640]{1,0:T(8,128)(2,1)S(1)} %copy-done), kind=kOutput, calls=%fused_computation.12 | convolution fusion | flops 3355443200 | bytes 11141120 | tf_op jit(solution)/shard_map/dot_general | solution.py:20
  132.2 0.0 all-reduce.3.cloned.1.call-update
  132.3 0.2 reduce-scatter.2.cloned.1.call-start
  132.5 110.4 %all-reduce.3.cloned.1.call-done = (f32[1024,640]{1,0:T(8,128)}, f32[1024,640]{1,0:T(8,128)}) async-done(((f32[1024,640]{1,0:T(8,128)}, f32[1024,640]{1,0:T(8,128)}), (f32[1024,640]{1,0:T(8,128)}, f32[1024,640]{1,0:T(8,128)})) %all-reduce.3.cloned.1.call-update) | async-done | bytes 5242896 | tf_op jit(solution)/shard_map/psum | solution.py:24
  242.9 3.1 fusion.5
  245.9 0.0 copy-start.1
  246.0 1.0 copy-done.1
  247.0 6.9 %fusion.9 = f32[1024,2560]{1,0:T(8,128)} fusion(bf16[1024,640]{1,0:T(8,128)(2,1)S(1)} %fusion.5, bf16[2560,640]{1,0:T(8,128)(2,1)S(1)} %copy-done), kind=kOutput, calls=%fused_computation.13 | convolution fusion | flops 3355443200 | bytes 15073280 | tf_op jit(solution)/shard_map/dot_general | solution.py:33
  253.9 0.0 reduce-scatter.2.cloned.1.call-update
  254.0 9.3 %convolution_bitcast_fusion = f32[2560,640]{0,1:T(8,128)} fusion(bf16[1024,640]{1,0:T(8,128)(2,1)} %copy-done.1, bf16[1024,2560]{1,0:T(8,128)(2,1)} %all-gather.5.cloned.1.call-done), kind=kOutput, calls=%fused_computation | convolution fusion | flops 3355443200 | bytes 13107200 | tf_op jit(solution)/shard_map/dot_general | solution.py:26
  263.2 8.3 %copy.7 = f32[2560,640]{1,0:T(8,128)} copy(f32[2560,640]{0,1:T(8,128)} %convolution_bitcast_fusion) | data formatting | bytes 13107200
  271.5 9.7 %fusion.6 = f32[640,2560]{1,0:T(8,128)} fusion(bf16[1024,2560]{1,0:T(8,128)(2,1)} %all-gather.3.cloned.1.call-done, f32[1024,640]{1,0:T(8,128)} %get-tuple-element.7), kind=kOutput, calls=%fused_computation.10 | convolution fusion | flops 3358720000 | bytes 14417920 | tf_op jit(solution)/shard_map/dot_general | solution.py:29
  281.2 149.2 %reduce-scatter.2.cloned.1.call-done = f32[32,2560]{1,0:T(8,128)} async-done(((f32[1024,2560]{1,0:T(8,128)}), f32[32,2560]{1,0:T(8,128)}) %reduce-scatter.2.cloned.1.call-update) | async-done | bytes 327696 | tf_op jit(solution)/shard_map/reduce_scatter | solution.py:32
  430.4 1.7 convert_element_type.10
Async XLA Ops:
  7.2 116.9 %copy-start = (bf16[2560,640]{1,0:T(8,128)(2,1)S(1)}, bf16[2560,640]{1,0:T(8,128)(2,1)}, u32[]{:S(2)}) copy-start(bf16[2560,640]{1,0:T(8,128)(2,1)} %param.6) | copy-start | bytes 9830404
  7.2 59.0 %all-gather.3.cloned.1.call-start = ((), (), s32[]{:S(2)}) async-start(), calls=%async_computation.1 | async-start | bytes 6553600 | tf_op jit(solution)/shard_map/all_gather | solution.py:18
  7.9 116.1 %all-gather.5.cloned.1.call-start = ((), (), s32[]{:S(2)}) async-start(), calls=%async_computation.2 | async-start | bytes 6553600 | tf_op jit(solution)/shard_map/all_gather | solution.py:17
  8.7 234.2 %all-reduce.3.cloned.1.call-start = ((), (), s32[]{:S(2)}) async-start(), calls=%async_computation.4 | async-start | bytes 10485760 | tf_op jit(solution)/shard_map/psum | solution.py:24
  132.3 298.1 %reduce-scatter.2.cloned.1.call-start = ((), (), s32[]{:S(2)}) async-start(), calls=%async_computation.3 | async-start | bytes 10813440 | tf_op jit(solution)/shard_map/reduce_scatter | solution.py:32
  245.9 1.1 copy-start.1
Sparse Core Ops, SparseCore 0:
  9.6 56.4 all-gather.2
  67.8 56.1 all-gather.4
  132.4 110.4 all-reduce.2
  254.1 176.2 reduce-scatter.1
where the time goes:
time: 439 us
  waiting for transfers between devices  367 us (84%)
  matrix products  43.4 us (10%)
  between operations  13.8 us (3%)
  local copies, waits for them, and re-layouts  9.32 us (2%)
  other arithmetic  4.71 us (1%)
    reduce_scatter x1, waiting for transfers between devices, per_device(): lax.psum_scatter(lax.dot_general(pre_grad, weight_in, (((1,), (1,)), ((),...  149 us
    psum x1, waiting for transfers between devices, per_device(): pre, act_grad = lax.psum((pre_part, grad_part), 'con')  110 us
    all_gather x1, waiting for transfers between devices, per_device(): lax.all_gather(out_grad, 'tok', axis=0, tiled=True)  57.5 us
    all_gather x1, waiting for transfers between devices, per_device(): lax.all_gather(tokens, 'tok', axis=0, tiled=True)  48.6 us
    dot_general x1, matrix products, per_device(): lax.dot_general(activ, gathered_grad, (((0,), (0,)), ((), ())), preferred...  9.72 us
    unnamed x5, local copies, waits for them, and re-layouts  9.32 us
    dot_general x1, matrix products, per_device(): lax.dot_general(gathered_tok, pre_grad, (((0,), (0,)), ((), ())), preferr...  9.29 us
    dot_general x1, matrix products, per_device(): lax.dot_general(gathered_grad, weight_out, (((1,), (1,)), ((), ())), pref...  9.24 us
  transfers between devices with their start and end apart: 4, of which 4 were waited for; matrix products, arithmetic and copies ran while one was open for 8% of the time, Pallas kernels for 0%

commit v1 on v0

v1 whole, which is shorter than its diff:
```python
import jax
import jax.numpy as jnp
from jax import lax
from jax.experimental import pallas as pl
from jax.experimental.pallas import tpu as pltpu
from jax.sharding import PartitionSpec as P

INTERPRET = False
AXES = ("tok", "con", "out")
BF, F32 = jnp.bfloat16, jnp.float32


def index_of(x, y, z, k):
    return (((z % 2) * 2 + k) * 4 + x) * 8 + (z // 2) * 4 + y


def shift(v, x=0, y=0, z=0, k=0):
    r = range(4)
    pairs = [
        (index_of(a, b, c, d), index_of((a + x) % 4, (b + y) % 4, (c + z) % 4, (d + k) % 2))
        for a in r for b in r for c in r for d in range(2)
    ]
    return lax.ppermute(v, AXES, pairs)


def gelu_parts(pre, act_grad):
    cdf = 0.5 * (1.0 + jax.scipy.special.erf(pre * 0.7071067811865476))
    density = jnp.exp(-0.5 * pre * pre) * 0.3989422804014327
    activ = (pre * cdf).astype(BF)
    pre_grad = (act_grad * (cdf + pre * density)).astype(BF)
    return (activ, pre_grad)


def run(body, outs, scal, args, scratch=(), flops=0, room=4 << 20):
    vmem = pl.BlockSpec(memory_space=pltpu.VMEM)
    shapes = [jax.ShapeDtypeStruct(*o) for o in outs]
    nbytes = sum(v.size * v.dtype.itemsize for v in [*args, *shapes])
    return pl.pallas_call(
        body,
        in_specs=[pl.BlockSpec(memory_space=pltpu.SMEM)] + [vmem] * len(args),
        out_specs=[vmem] * len(outs),
        out_shape=shapes,
        scratch_shapes=list(scratch),
        cost_estimate=pl.CostEstimate(flops=flops, bytes_accessed=nbytes, transcendentals=0),
        compiler_params=pltpu.CompilerParams(vmem_limit_bytes=nbytes + room),
        interpret=INTERPRET,
    )(scal, *args)


def product(a, b, ca, cb):
    return lax.dot_general(a, b, (((ca,), (cb,)), ((), ())), preferred_element_type=F32)


def cat(refs):
    return refs[0][...] if len(refs) == 1 else jnp.concatenate([r[...] for r in refs], axis=0)


def project(scal, jobs):
    args, flops = [], 0
    for blocks, w, _ in jobs:
        args += [*blocks, w]
        flops += 2 * sum(v.shape[0] for v in blocks) * w.size
    rows = sum(v.shape[0] for v in jobs[0][0])
    hidden = jobs[0][1].shape[1 - jobs[0][2]]
    quarter = rows // 8

    def body(s, *refs):
        x = s[0]
        outs, keep, part = refs[-5:-2], refs[-2], refs[-1]
        at = 0
        for a, (blocks, _, dim) in enumerate(jobs):
            lhs = cat(refs[at : at + len(blocks)])
            w = refs[at + len(blocks)]
            at += len(blocks) + 1
            part[...] = product(lhs, w[...], 1, dim)
            for b in range(2):
                for o, j in zip(outs, (1, 3, 2)):
                    o[a, b] = part[pl.ds(b * 4 * quarter + lax.rem(x + j, 4) * quarter, quarter), :].astype(BF)
                keep[a, b] = part[pl.ds(b * 4 * quarter + x * quarter, quarter), :]

    shape = (len(jobs), 2, quarter, hidden)
    *sent, keep = run(
        body, [(shape, BF)] * 3 + [(shape, F32)], scal, args, [pltpu.VMEM((rows, hidden), F32)], flops, 12 << 20)
    return sent, keep


def back(scal, parts, pick, w):
    width = w.shape[0]
    quarter, hidden = parts[0].shape[-2:]
    tile = 512 if width % 512 == 0 else 128

    def body(s, p0, p1, p2, p3, w_ref, other, mine):
        x = s[0]
        lhs = jnp.concatenate([pick(p)[b] for b in range(2) for p in (p0, p1, p2, p3)], axis=0)
        for t in range(0, width, tile):
            res = product(lhs, w_ref[t : t + tile, :], 1, 1)
            for j in range(4):
                at = pl.ds(lax.rem(x + 4 - j, 4) * quarter, quarter)
                mine[at, t : t + tile] = res[j * quarter : (j + 1) * quarter]
                other[at, t : t + tile] = res[(4 + j) * quarter : (5 + j) * quarter].astype(BF)

    return run(
        body, [((4 * quarter, width), BF), ((4 * quarter, width), F32)], scal, [*parts, w],
        flops=16 * quarter * hidden * width, room=8 << 20)


def weight_grad(scal, lefts, rights, pick, tile_left):
    blocks, parts = (lefts, rights) if tile_left else (rights, lefts)
    width = blocks[0].shape[1]
    quarter, hidden = parts[0].shape[-2:]
    tile = 512 if width % 512 == 0 else 128
    rows = sum(v.shape[0] for v in blocks)

    def body(s, *refs):
        x = s[0]
        wide, quarters, out, held = refs[: len(blocks)], refs[len(blocks) : -2], refs[-2], refs[-1]

        @pl.when(pl.program_id(0) == 0)
        def _():
            for c, j, b in [(c, j, b) for c in range(2) for j in range(4) for b in range(2)]:
                at = pl.ds((2 * c + b) * 4 * quarter + lax.rem(x + 4 - j, 4) * quarter, quarter)
                held[at, :] = pick(quarters, c, j)[b]

        a, b = cat(wide), held[...]
        out[...] = product(a, b, 0, 0) if tile_left else product(b, a, 0, 0)

    shape = (width, hidden) if tile_left else (hidden, width)
    block = (tile, hidden) if tile_left else (hidden, tile)
    return pl.pallas_call(
        body,
        grid=(width // tile,),
        in_specs=[pl.BlockSpec(memory_space=pltpu.SMEM)]
        + [pl.BlockSpec((v.shape[0], tile), lambda i: (0, i)) for v in blocks]
        + [pl.BlockSpec(v.shape, lambda i, n=v.ndim: (0,) * n) for v in parts],
        out_specs=pl.BlockSpec(block, (lambda i: (i, 0)) if tile_left else (lambda i: (0, i))),
        out_shape=jax.ShapeDtypeStruct(shape, F32),
        scratch_shapes=[pltpu.VMEM((rows, hidden), BF)],
        cost_estimate=pl.CostEstimate(
            flops=2 * rows * width * hidden, bytes_accessed=2 * rows * (width + hidden) + 4 * width * hidden,
            transcendentals=0),
        compiler_params=pltpu.CompilerParams(vmem_limit_bytes=20 << 20),
        interpret=INTERPRET,
    )(scal, *blocks, *parts)


def f32(v):
    return v.astype(F32)


def gelu(scal, own, got, picks, before=None):
    shape = own[0].shape[1:]

    def body(s, *refs):
        n = len(own)
        keep, pieces, (activ, pre_grad) = refs[:n], refs[n : n + len(got)], refs[-2:]
        both = []
        for src, at in picks:
            p = pieces[3 * src : 3 * src + 3]
            both.append(keep[src][at] + (f32(p[0][at]) + f32(p[1][at]) + f32(p[2][at])))
        if before is None:
            activ[...], pre_grad[...] = gelu_parts(*both)
        else:
            activ[0] = refs[-3][...]
            activ[1], pre_grad[...] = gelu_parts(*both)

    more = [] if before is None else [before]
    return run(body, [((2,) * len(more) + shape, BF), (shape, BF)], scal, [*own, *got, *more])


def cut(scal, v):
    n = v.shape[0] // 2

    def body(s, v, a, b):
        a[...] = v[:n]
        b[...] = v[n:]

    return run(body, [((n, v.shape[1]), BF)] * 2, scal, [v], room=1 << 20)


def body_of(tokens, out_grad, weight_in, weight_out):
    ix = lax.axis_index("con")
    it, io = lax.axis_index("tok"), lax.axis_index("out")
    zl, zh, iy = it >> 1, io >> 2, io & 3
    scal = jnp.stack([ix, iy, zh, zh ^ zl]).astype(jnp.int32)
    rows, width = tokens.shape
    half, small = width // 2, rows // 8
    whole = lambda v: v[...]

    def around(sent, name):
        return [shift(v, **{name: j}) for v, j in zip(sent, (1, 3, 2))]

    def spread(v):
        return [v] + [shift(v, x=j) for j in (1, 2, 3)]

    partner, top = [], []
    for v in (tokens, out_grad):
        partner.append(shift(v, k=1))
        up, down = cut(scal, v)
        top.append([shift(up, z=3), shift(down, z=1)])
    sent_l, keep_l = project(
        scal, [((tokens, partner[0]), weight_in, 0), ((out_grad, partner[1]), weight_out, 1)])
    got_l = around(sent_l, "x")
    far_t = top[0] + [shift(v, k=1) for v in top[0]]
    sent_r, keep_r = project(scal, [(far_t, weight_in, 0)])
    got_r = around(sent_r, "x")
    ac_l, pg_l = gelu(scal, [keep_l], got_l, ((0, 0), (0, 1)))
    pg_l = spread(pg_l)

    far_g = top[1] + [shift(v, k=1) for v in top[1]]
    sent_g, keep_g = project(scal, [(far_g, weight_out, 1)])
    got_g = around(sent_g, "x")

    other_l, mine_l = back(scal, pg_l, whole, weight_in)
    swapped_l = shift(other_l, k=1)
    activ_q, pre_grad_q = gelu(scal, [keep_r, keep_g], [*got_r, *got_g], ((0, 0), (1, 0)), ac_l)
    pg_r = spread(pre_grad_q)
    activ = spread(activ_q)

    def mid_l(s, mine, got, send, keep):
        n = 4 * small
        a, b = pl.ds(s[2] * n, n), pl.ds((1 - s[2]) * n, n)
        keep[...] = mine[a, :] + f32(got[a, :])
        send[...] = (mine[b, :] + f32(got[b, :])).astype(BF)

    send, keep = run(
        mid_l, [((4 * small, width), BF), ((4 * small, width), F32)], scal, [mine_l, swapped_l])
    other = shift(send, z=2)

    other_r, mine_r = back(scal, pg_r, whole, weight_in)
    swapped_r = shift(other_r, k=1)

    def mid_r(s, mine, got, o1, o3, o2, stay, up, down):
        for g in range(2):
            for o, j in ((o1, 1), (o3, 3), (o2, 2)):
                at = pl.ds((g * 4 + lax.rem(s[1] + j, 4)) * small, small)
                o[g] = (mine[at, :half] + f32(got[at, :half])).astype(BF)
            at = pl.ds((g * 4 + s[1]) * small, small)
            stay[g] = mine[at, :half] + f32(got[at, :half])
        n = 4 * small
        for o, g in ((up, s[3]), (down, 1 - s[3])):
            at = pl.ds(g * n, n)
            o[...] = (mine[at, half:] + f32(got[at, half:])).astype(BF)

    group, part = (2, small, half), (4 * small, half)
    *send, stay, up, down = run(
        mid_r, [(group, BF)] * 3 + [(group, F32)] + [(part, BF)] * 2, scal, [mine_r, swapped_r])
    got_a = around(send, "y")
    got_b = [shift(up, z=1), shift(down, z=3)]
    first_grad = weight_grad(
        scal, [tokens, partner[0], *far_t], [*pg_l, *pg_r], lambda v, c, j: v[4 * c + j], True)

    def next_r(s, stay, a1, a3, a2, b0, b1, kept, got, up, down, o1, o3, o2, own):
        for o, g in ((up, s[3]), (down, 1 - s[3])):
            o[...] = (stay[g] + (f32(a1[g]) + f32(a3[g]) + f32(a2[g]))).astype(BF)
        for o, j in ((o1, 1), (o3, 3), (o2, 2), (own, 0)):
            at = pl.ds(lax.rem(s[1] + j, 4) * small, small)
            v = kept[at, :] + f32(got[at, :])
            o[:, :half] = v[:, :half].astype(o.dtype)
            o[:, half:] = (v[:, half:] + (f32(b0[at, :]) + f32(b1[at, :]))).astype(o.dtype)

    up, down, *send, own = run(
        next_r, [((small, half), BF)] * 2 + [((small, width), BF)] * 3 + [((small, width), F32)], scal,
        [stay, *got_a, *got_b, keep, other])
    got_a = [shift(up, z=1), shift(down, z=3)]
    got_b = around(send, "y")
    second_grad = weight_grad(
        scal, activ, [out_grad, partner[1], *far_g], lambda v, c, j: v[j].at[c], False)

    def last(s, own, b1, b3, b2, a0, a1, out):
        v = own[...] + (f32(b1[...]) + f32(b3[...]) + f32(b2[...]))
        out[:, :half] = (v[:, :half] + (f32(a0[...]) + f32(a1[...]))).astype(BF)
        out[:, half:] = v[:, half:].astype(BF)

    (input_grad,) = run(last, [((small, width), BF)], scal, [own, *got_b, *got_a])
    return (input_grad, first_grad, second_grad)


def solution(mesh):
    placed = (P("tok", "con"), P("tok", "con"), P("con", ("tok", "out")), P(("tok", "out"), "con"))
    return jax.shard_map(
        body_of,
        mesh=mesh,
        in_specs=placed,
        out_specs=(P(("tok", "out"), "con"), P("con", ("tok", "out")), P(("tok", "out"), "con")),
        check_vma=False,
    )
```

time: 439 us -> 155 us (0.35)
  the two profiles are of different devices: /device:TPU:26 before, /device:TPU:0 now
where the time goes in v1:
time: 155 us
  waiting for transfers between devices  60.2 us (39%)
  starting transfers between devices  50.9 us (33%)
  Pallas kernels  38.8 us (25%)
  local copies, waits for them, and re-layouts  3.86 us (2%)
    ppermute x41, waiting for transfers between devices, shift(): return lax.ppermute(v, AXES, pairs)  60.2 us
    ppermute x41, starting transfers between devices, shift(): return lax.ppermute(v, AXES, pairs)  50.9 us
    pallas_call x13, Pallas kernels, run(): pl.pallas_call(body, in_specs=[pl.BlockSpec(memory_space=pltpu.SMEM)] + [...  24.5 us
    pallas_call x2, Pallas kernels, weight_grad(): pl.pallas_call(body, grid=(width // tile,), in_specs=[pl.BlockSpec(memory...  14.2 us
    unnamed x8, local copies, waits for them, and re-layouts  3.86 us
  transfers between devices with their start and end apart: 41, of which 16 were waited for; matrix products, arithmetic and copies ran while one was open for 0% of the time, Pallas kernels for 23%

profile of v1, /device:TPU:0, one launch (start us, length us, event | category | flops | bytes accessed | tf_op | source)
XLA Modules:
  0.0 154.7 jit_solution(9490345099698398403)
XLA Ops:
  0.7 1.5 shard_map.67
  2.2 4.2 %collective-permute-start = (bf16[128,2560]{1,0:T(8,128)(2,1)S(1)}, bf16[128,2560]{1,0:T(8,128)(2,1)S(1)}, u32[]{:S(2)}, u32[]{:S(2)}) collective-permute-start(bf16[128,2560]{1,0:T(8,128)(2,1)S(1)} %get-tuple-element.41), channel_id=1, source_target_pairs={{0,68},{32,100},{64,0},{96,32},{4,64},{36,96},{68,4},{100,36},{1,6... | collective-permute-start | bytes 1966088 | tf_op jit(solution)/shard_map/ppermute | solution.py:23
  6.5 0.5 collective-permute-start.15
  7.0 0.6 shard_map.69
  7.6 3.3 %collective-permute-start.4 = (bf16[128,2560]{1,0:T(8,128)(2,1)S(1)}, bf16[128,2560]{1,0:T(8,128)(2,1)S(1)}, u32[]{:S(2)}, u32[]{:S(2)}) collective-permute-start(bf16[128,2560]{1,0:T(8,128)(2,1)S(1)} %get-tuple-element.44), channel_id=1, source_target_pairs={{0,68},{32,100},{64,0},{96,32},{4,64},{36,96},{68,4},{100,36},{1,6... | collective-permute-start | bytes 1966088 | tf_op jit(solution)/shard_map/ppermute | solution.py:23
  10.9 10.7 %collective-permute-done.refs_0_.refs_2_ = bf16[128,2560]{1,0:T(8,128)(2,1)S(1)} collective-permute-done((bf16[128,2560]{1,0:T(8,128)(2,1)S(1)}, bf16[128,2560]{1,0:T(8,128)(2,1)S(1)}, u32[]{:S(2)}, u32[]{:S(2)}) %collective-permute-start) | collective-permute-done | bytes 655392 | tf_op jit(solution)/shard_map/ppermute | solution.py:23
  21.6 0.4 collective-permute-start.5
  21.9 3.7 %collective-permute-done.1.refs_1_.refs_3_ = bf16[128,2560]{1,0:T(8,128)(2,1)S(1)} collective-permute-done((bf16[128,2560]{1,0:T(8,128)(2,1)S(1)}, bf16[128,2560]{1,0:T(8,128)(2,1)S(1)}, u32[]{:S(2)}, u32[]{:S(2)}) %collective-permute-start.1) | collective-permute-done | bytes 655392 | tf_op jit(solution)/shard_map/ppermute | solution.py:23
  25.7 8.8 %collective-permute-done.4.refs_0_.refs_2_ = bf16[128,2560]{1,0:T(8,128)(2,1)S(1)} collective-permute-done((bf16[128,2560]{1,0:T(8,128)(2,1)S(1)}, bf16[128,2560]{1,0:T(8,128)(2,1)S(1)}, u32[]{:S(2)}, u32[]{:S(2)}) %collective-permute-start.4) | collective-permute-done | bytes 655392 | tf_op jit(solution)/shard_map/ppermute | solution.py:23
  34.5 4.4 %collective-permute-done.5.refs_1_.refs_3_ = bf16[128,2560]{1,0:T(8,128)(2,1)S(1)} collective-permute-done((bf16[128,2560]{1,0:T(8,128)(2,1)S(1)}, bf16[128,2560]{1,0:T(8,128)(2,1)S(1)}, u32[]{:S(2)}, u32[]{:S(2)}) %collective-permute-start.5) | collective-permute-done | bytes 655392 | tf_op jit(solution)/shard_map/ppermute | solution.py:23
  38.9 0.5 collective-permute-start.7
  39.4 1.9 %copy-done.1 = bf16[640,2560]{1,0:T(8,128)(2,1)S(1)} copy-done((bf16[640,2560]{1,0:T(8,128)(2,1)S(1)}, bf16[640,2560]{1,0:T(8,128)(2,1)}, u32[]{:S(2)}) %copy-start.1) | copy-done | bytes 3276824
  41.3 1.9 %copy-done.2 = bf16[2560,640]{1,0:T(8,128)(2,1)S(1)} copy-done((bf16[2560,640]{1,0:T(8,128)(2,1)S(1)}, bf16[2560,640]{1,0:T(8,128)(2,1)}, u32[]{:S(2)}) %copy-start.2) | copy-done | bytes 3276824
  43.2 5.8 %shard_map.71 = (bf16[2,2,64,640]{3,2,1,0:T(8,128)(2,1)S(1)}, bf16[2,2,64,640]{3,2,1,0:T(8,128)(2,1)S(1)}, bf16[2,2,64,640]{3,2,1,0:T(8,128)(2,1)S(1)}, f32[2,2,64,640]{3,2,1,0:T(8,128)S(1)}) custom-call(s32[4]{0:T(128)S(1)} %pad_add_fusion.s, bf16[256,2560]{1,0:T(8,128)(2,1)} %refs_0_.4, bf16[256,2560]{1,0:T(8,128)(2,1)S(1)} %collective-permute-done.14.refs_1_, ...), custom_call_target="tpu_custom_call" | custom-call | flops 3355443200 | bytes 13434880 | tf_op jit(solution)/shard_map/pallas_call | solution.py:38
  49.0 1.6 %collective-permute-start.16 = (bf16[2,2,64,640]{3,2,1,0:T(8,128)(2,1)S(1)}, bf16[2,2,64,640]{3,2,1,0:T(8,128)(2,1)S(1)}, u32[]{:S(2)}, u32[]{:S(2)}) collective-permute-start(bf16[2,2,64,640]{3,2,1,0:T(8,128)(2,1)S(1)} %get-tuple-element.54), channel_id=1, source_target_pairs={{0,8},{32,40},{64,72},{96,104},{4,12},{36,44},{68,76},{100,108},{1... | collective-permute-start | bytes 983048 | tf_op jit(solution)/shard_map/ppermute | solution.py:23
  50.6 1.7 %collective-permute-start.17 = (bf16[2,2,64,640]{3,2,1,0:T(8,128)(2,1)S(1)}, bf16[2,2,64,640]{3,2,1,0:T(8,128)(2,1)S(1)}, u32[]{:S(2)}, u32[]{:S(2)}) collective-permute-start(bf16[2,2,64,640]{3,2,1,0:T(8,128)(2,1)S(1)} %get-tuple-element.55), channel_id=1, source_target_pairs={{0,24},{32,56},{64,88},{96,120},{4,28},{36,60},{68,92},{100,124},{... | collective-permute-start | bytes 983048 | tf_op jit(solution)/shard_map/ppermute | solution.py:23
  52.4 1.8 %collective-permute-start.18 = (bf16[2,2,64,640]{3,2,1,0:T(8,128)(2,1)S(1)}, bf16[2,2,64,640]{3,2,1,0:T(8,128)(2,1)S(1)}, u32[]{:S(2)}, u32[]{:S(2)}) collective-permute-start(bf16[2,2,64,640]{3,2,1,0:T(8,128)(2,1)S(1)} %get-tuple-element.56), channel_id=1, source_target_pairs={{0,16},{32,48},{64,80},{96,112},{4,20},{36,52},{68,84},{100,116},{... | collective-permute-start | bytes 983048 | tf_op jit(solution)/shard_map/ppermute | solution.py:23
  54.2 2.8 %shard_map.68 = (bf16[1,2,64,640]{3,2,1,0:T(8,128)(2,1)S(1)}, bf16[1,2,64,640]{3,2,1,0:T(8,128)(2,1)S(1)}, bf16[1,2,64,640]{3,2,1,0:T(8,128)(2,1)S(1)}, f32[1,2,64,640]{3,2,1,0:T(8,128)S(1)}) custom-call(s32[4]{0:T(128)S(1)} %pad_add_fusion.s, bf16[128,2560]{1,0:T(8,128)(2,1)S(1)} %collective-permute-done.refs_0_.refs_2_, ...), custom_call_target="tpu_custom_call" | custom-call | flops 1677721600 | bytes 6717440 | tf_op jit(solution)/shard_map/pallas_call | solution.py:38
  57.0 0.7 collective-permute-start.8
  57.7 2.6 %collective-permute-start.9 = (bf16[1,2,64,640]{3,2,1,0:T(8,128)(2,1)S(1)}, bf16[1,2,64,640]{3,2,1,0:T(8,128)(2,1)S(1)}, u32[]{:S(2)}, u32[]{:S(2)}) collective-permute-start(bf16[1,2,64,640]{3,2,1,0:T(8,128)(2,1)S(1)} %get-tuple-element.48), channel_id=1, source_target_pairs={{0,24},{32,56},{64,88},{96,120},{4,28},{36,60},{68,92},{100,124},{... | collective-permute-start | bytes 491528 | tf_op jit(solution)/shard_map/ppermute | solution.py:23
  60.4 2.8 %shard_map.70 = (bf16[1,2,64,640]{3,2,1,0:T(8,128)(2,1)S(1)}, bf16[1,2,64,640]{3,2,1,0:T(8,128)(2,1)S(1)}, bf16[1,2,64,640]{3,2,1,0:T(8,128)(2,1)S(1)}, f32[1,2,64,640]{3,2,1,0:T(8,128)S(1)}) custom-call(s32[4]{0:T(128)S(1)} %pad_add_fusion.s, bf16[128,2560]{1,0:T(8,128)(2,1)S(1)} %collective-permute-done.4.refs_0_.refs_2_, ...), custom_call_target="tpu_custom_call" | custom-call | flops 1677721600 | bytes 6717440 | tf_op jit(solution)/shard_map/pallas_call | solution.py:38
  63.2 7.3 %collective-permute-done.8.refs_2_ = bf16[1,2,64,640]{3,2,1,0:T(8,128)(2,1)S(1)} collective-permute-done((bf16[1,2,64,640]{3,2,1,0:T(8,128)(2,1)S(1)}, bf16[1,2,64,640]{3,2,1,0:T(8,128)(2,1)S(1)}, u32[]{:S(2)}, u32[]{:S(2)}) %collective-permute-start.8) | collective-permute-done | bytes 163872 | tf_op jit(solution)/shard_map/ppermute | solution.py:23
  70.6 1.7 %collective-permute-start.10 = (bf16[1,2,64,640]{3,2,1,0:T(8,128)(2,1)S(1)}, bf16[1,2,64,640]{3,2,1,0:T(8,128)(2,1)S(1)}, u32[]{:S(2)}, u32[]{:S(2)}) collective-permute-start(bf16[1,2,64,640]{3,2,1,0:T(8,128)(2,1)S(1)} %get-tuple-element.49), channel_id=1, source_target_pairs={{0,16},{32,48},{64,80},{96,112},{4,20},{36,52},{68,84},{100,116},{... | collective-permute-start | bytes 491528 | tf_op jit(solution)/shard_map/ppermute | solution.py:23
  72.3 0.6 collective-permute-start.11
  72.9 2.6 %collective-permute-start.12 = (bf16[1,2,64,640]{3,2,1,0:T(8,128)(2,1)S(1)}, bf16[1,2,64,640]{3,2,1,0:T(8,128)(2,1)S(1)}, u32[]{:S(2)}, u32[]{:S(2)}) collective-permute-start(bf16[1,2,64,640]{3,2,1,0:T(8,128)(2,1)S(1)} %get-tuple-element.51), channel_id=1, source_target_pairs={{0,24},{32,56},{64,88},{96,120},{4,28},{36,60},{68,92},{100,124},{... | collective-permute-start | bytes 491528 | tf_op jit(solution)/shard_map/ppermute | solution.py:23
  75.5 0.6 collective-permute-start.13
  76.1 0.8 shard_map.72
  77.0 0.6 collective-permute-start.28
  77.6 1.5 collective-permute-done.10.refs_4_
  79.1 1.8 %collective-permute-start.29 = (bf16[2,64,640]{2,1,0:T(8,128)(2,1)S(1)}, bf16[2,64,640]{2,1,0:T(8,128)(2,1)S(1)}, u32[]{:S(2)}, u32[]{:S(2)}) collective-permute-start(bf16[2,64,640]{2,1,0:T(8,128)(2,1)S(1)} %get-tuple-element.67.p0.refs_6_), channel_id=1, source_target_pairs={{0,16},{32,48},{64,80},{96,112},{4,20},{36,52},{68,84},{100,116},{... | collective-permute-start | bytes 491528 | tf_op jit(solution)/shard_map/ppermute | solution.py:23
  80.9 3.2 %collective-permute-done.11.refs_5_ = bf16[1,2,64,640]{3,2,1,0:T(8,128)(2,1)S(1)} collective-permute-done((bf16[1,2,64,640]{3,2,1,0:T(8,128)(2,1)S(1)}, bf16[1,2,64,640]{3,2,1,0:T(8,128)(2,1)S(1)}, u32[]{:S(2)}, u32[]{:S(2)}) %collective-permute-start.11) | collective-permute-done | bytes 163872 | tf_op jit(solution)/shard_map/ppermute | solution.py:23
  84.1 1.1 collective-permute-done.12.refs_6_
  85.2 0.9 collective-permute-done.13.refs_7_
  86.2 0.9 shard_map.73
  87.0 0.3 collective-permute-start.19
  87.3 4.5 %collective-permute-start.20 = (bf16[2,64,640]{2,1,0:T(8,128)(2,1)S(1)}, bf16[2,64,640]{2,1,0:T(8,128)(2,1)S(1)}, u32[]{:S(2)}, u32[]{:S(2)}) collective-permute-start(bf16[2,64,640]{2,1,0:T(8,128)(2,1)S(1)} %get-tuple-element.58.p0.refs_10_), channel_id=1, source_target_pairs={{0,16},{32,48},{64,80},{96,112},{4,20},{36,52},{68,84},{100,116},{... | collective-permute-start | bytes 491528 | tf_op jit(solution)/shard_map/ppermute | solution.py:23
  91.8 1.3 collective-permute-done.29.p2.refs_8_
  93.2 2.8 %shard_map.76 = (bf16[256,2560]{1,0:T(8,128)(2,1)S(1)}, f32[256,2560]{1,0:T(8,128)S(1)}) custom-call(s32[4]{0:T(128)S(1)} %pad_add_fusion.s, bf16[2,64,640]{2,1,0:T(8,128)(2,1)S(1)} %get-tuple-element.67.p0.refs_6_, bf16[2,64,640]{2,1,0:T(8,128)(2,1)S(1)} %collective-permute-done.28.p1.refs_7_, bf16[2,64,640]{2,1,0:T(8,128)(2,1)S(1)} %collective-permute-done.29.p2.refs_8_, ...), custom_call_target="tpu_custom_call" | custom-call | flops 1677721600 | bytes 7864320 | tf_op jit(solution)/shard_map/pallas_call | solution.py:38
  96.0 0.1 collective-permute-start.31
  96.1 0.6 collective-permute-done.19.p1.refs_11_
  96.7 1.8 %collective-permute-done.20.p2.refs_12_ = bf16[2,64,640]{2,1,0:T(8,128)(2,1)S(1)} collective-permute-done((bf16[2,64,640]{2,1,0:T(8,128)(2,1)S(1)}, bf16[2,64,640]{2,1,0:T(8,128)(2,1)S(1)}, u32[]{:S(2)}, u32[]{:S(2)}) %collective-permute-start.20) | collective-permute-done | bytes 163872 | tf_op jit(solution)/shard_map/ppermute | solution.py:23
  98.4 2.8 %shard_map.74 = (bf16[256,2560]{1,0:T(8,128)(2,1)S(1)}, f32[256,2560]{1,0:T(8,128)S(1)}) custom-call(s32[4]{0:T(128)S(1)} %pad_add_fusion.s, bf16[2,64,640]{2,1,0:T(8,128)(2,1)S(1)} %get-tuple-element.58.p0.refs_10_, bf16[2,64,640]{2,1,0:T(8,128)(2,1)S(1)} %collective-permute-done.19.p1.refs_11_, ...), custom_call_target="tpu_custom_call" | custom-call | flops 1677721600 | bytes 7864320 | tf_op jit(solution)/shard_map/pallas_call | solution.py:38
  101.4 0.8 shard_map.77
  102.1 0.1 collective-permute-start.32
  102.2 2.1 %collective-permute-done.22.got = bf16[256,2560]{1,0:T(8,128)(2,1)S(1)} collective-permute-done((bf16[256,2560]{1,0:T(8,128)(2,1)S(1)}, bf16[256,2560]{1,0:T(8,128)(2,1)S(1)}, u32[]{:S(2)}, u32[]{:S(2)}) %collective-permute-start.22) | collective-permute-done | bytes 1310752 | tf_op jit(solution)/shard_map/ppermute | solution.py:23
  104.4 0.8 shard_map.75
  105.2 1.6 %collective-permute-start.23 = (bf16[2,32,1280]{2,1,0:T(8,128)(2,1)S(1)}, bf16[2,32,1280]{2,1,0:T(8,128)(2,1)S(1)}, u32[]{:S(2)}, u32[]{:S(2)}) collective-permute-start(bf16[2,32,1280]{2,1,0:T(8,128)(2,1)S(1)} %get-tuple-element.62), channel_id=1, source_target_pairs={{0,1},{32,33},{64,65},{96,97},{4,5},{36,37},{68,69},{100,101},{1,2... | collective-permute-start | bytes 491528 | tf_op jit(solution)/shard_map/ppermute | solution.py:23
  106.8 1.7 %collective-permute-start.24 = (bf16[2,32,1280]{2,1,0:T(8,128)(2,1)S(1)}, bf16[2,32,1280]{2,1,0:T(8,128)(2,1)S(1)}, u32[]{:S(2)}, u32[]{:S(2)}) collective-permute-start(bf16[2,32,1280]{2,1,0:T(8,128)(2,1)S(1)} %get-tuple-element.63), channel_id=1, source_target_pairs={{0,3},{32,35},{64,67},{96,99},{4,7},{36,39},{68,71},{100,103},{1,0... | collective-permute-start | bytes 491528 | tf_op jit(solution)/shard_map/ppermute | solution.py:23
  108.5 2.0 %collective-permute-start.25 = (bf16[2,32,1280]{2,1,0:T(8,128)(2,1)S(1)}, bf16[2,32,1280]{2,1,0:T(8,128)(2,1)S(1)}, u32[]{:S(2)}, u32[]{:S(2)}) collective-permute-start(bf16[2,32,1280]{2,1,0:T(8,128)(2,1)S(1)} %get-tuple-element.64), channel_id=1, source_target_pairs={{0,2},{32,34},{64,66},{96,98},{4,6},{36,38},{68,70},{100,102},{1,3... | collective-permute-start | bytes 491528 | tf_op jit(solution)/shard_map/ppermute | solution.py:23
  110.5 2.3 %collective-permute-done.23.a1 = bf16[2,32,1280]{2,1,0:T(8,128)(2,1)S(1)} collective-permute-done((bf16[2,32,1280]{2,1,0:T(8,128)(2,1)S(1)}, bf16[2,32,1280]{2,1,0:T(8,128)(2,1)S(1)}, u32[]{:S(2)}, u32[]{:S(2)}) %collective-permute-start.23) | collective-permute-done | bytes 163872 | tf_op jit(solution)/shard_map/ppermute | solution.py:23
  112.8 2.9 %collective-permute-start.27 = (bf16[128,1280]{1,0:T(8,128)(2,1)S(1)}, bf16[128,1280]{1,0:T(8,128)(2,1)S(1)}, u32[]{:S(2)}, u32[]{:S(2)}) collective-permute-start(bf16[128,1280]{1,0:T(8,128)(2,1)S(1)} %get-tuple-element.66), channel_id=1, source_target_pairs={{0,68},{32,100},{64,0},{96,32},{4,64},{36,96},{68,4},{100,36},{1,6... | collective-permute-start | bytes 983048 | tf_op jit(solution)/shard_map/ppermute | solution.py:23
  115.7 0.2 collective-permute-start.38
  115.9 1.6 %collective-permute-done.25.a2 = bf16[2,32,1280]{2,1,0:T(8,128)(2,1)S(1)} collective-permute-done((bf16[2,32,1280]{2,1,0:T(8,128)(2,1)S(1)}, bf16[2,32,1280]{2,1,0:T(8,128)(2,1)S(1)}, u32[]{:S(2)}, u32[]{:S(2)}) %collective-permute-start.25) | collective-permute-done | bytes 163872 | tf_op jit(solution)/shard_map/ppermute | solution.py:23
  117.5 1.7 %collective-permute-start.39 = (bf16[2,2,64,640]{3,2,1,0:T(8,128)(2,1)S(1)}, bf16[2,2,64,640]{3,2,1,0:T(8,128)(2,1)S(1)}, u32[]{:S(2)}, u32[]{:S(2)}) collective-permute-start(bf16[2,2,64,640]{3,2,1,0:T(8,128)(2,1)S(1)} %get-tuple-element.78.refs_6_), channel_id=1, source_target_pairs={{0,16},{32,48},{64,80},{96,112},{4,20},{36,52},{68,84},{100,116},{... | collective-permute-start | bytes 983048 | tf_op jit(solution)/shard_map/ppermute | solution.py:23
  119.2 8.7 %collective-permute-done.26.b0 = bf16[128,1280]{1,0:T(8,128)(2,1)S(1)} collective-permute-done((bf16[128,1280]{1,0:T(8,128)(2,1)S(1)}, bf16[128,1280]{1,0:T(8,128)(2,1)S(1)}, u32[]{:S(2)}, u32[]{:S(2)}) %collective-permute-start.26) | collective-permute-done | bytes 327712 | tf_op jit(solution)/shard_map/ppermute | solution.py:23
  127.9 1.9 %collective-permute-start.40 = (bf16[2,2,64,640]{3,2,1,0:T(8,128)(2,1)S(1)}, bf16[2,2,64,640]{3,2,1,0:T(8,128)(2,1)S(1)}, u32[]{:S(2)}, u32[]{:S(2)}) collective-permute-start(bf16[2,2,64,640]{3,2,1,0:T(8,128)(2,1)S(1)} %get-tuple-element.78.refs_6_), channel_id=1, source_target_pairs={{0,24},{32,56},{64,88},{96,120},{4,28},{36,60},{68,92},{100,124},{... | collective-permute-start | bytes 983048 | tf_op jit(solution)/shard_map/ppermute | solution.py:23
  129.8 7.6 %shard_map.80 = f32[2560,640]{1,0:T(8,128)} custom-call(s32[4]{0:T(128)S(1)} %pad_add_fusion.s, bf16[256,2560]{1,0:T(8,128)(2,1)} %refs_0_.4, bf16[256,2560]{1,0:T(8,128)(2,1)S(1)} %collective-permute-done.14.refs_1_, bf16[128,2560]{1,0:T(8,128)(2,1)S(1)} %collective-permute-done.refs_0_.refs_2_, ...), custom_call_target="tpu_custom_call" | custom-call | flops 3355443200 | bytes 13107200 | tf_op jit(solution)/shard_map/pallas_call | solution.py:129
  137.3 0.8 shard_map.78
  138.2 1.6 %collective-permute-start.33 = (bf16[32,2560]{1,0:T(8,128)(2,1)S(1)}, bf16[32,2560]{1,0:T(8,128)(2,1)S(1)}, u32[]{:S(2)}, u32[]{:S(2)}) collective-permute-start(bf16[32,2560]{1,0:T(8,128)(2,1)S(1)} %get-tuple-element.73), channel_id=1, source_target_pairs={{0,1},{32,33},{64,65},{96,97},{4,5},{36,37},{68,69},{100,101},{1,2... | collective-permute-start | bytes 491528 | tf_op jit(solution)/shard_map/ppermute | solution.py:23
  139.8 1.7 %collective-permute-start.34 = (bf16[32,2560]{1,0:T(8,128)(2,1)S(1)}, bf16[32,2560]{1,0:T(8,128)(2,1)S(1)}, u32[]{:S(2)}, u32[]{:S(2)}) collective-permute-start(bf16[32,2560]{1,0:T(8,128)(2,1)S(1)} %get-tuple-element.74), channel_id=1, source_target_pairs={{0,3},{32,35},{64,67},{96,99},{4,7},{36,39},{68,71},{100,103},{1,0... | collective-permute-start | bytes 491528 | tf_op jit(solution)/shard_map/ppermute | solution.py:23
  141.5 2.0 %collective-permute-start.35 = (bf16[32,2560]{1,0:T(8,128)(2,1)S(1)}, bf16[32,2560]{1,0:T(8,128)(2,1)S(1)}, u32[]{:S(2)}, u32[]{:S(2)}) collective-permute-start(bf16[32,2560]{1,0:T(8,128)(2,1)S(1)} %get-tuple-element.75), channel_id=1, source_target_pairs={{0,2},{32,34},{64,66},{96,98},{4,6},{36,38},{68,70},{100,102},{1,3... | collective-permute-start | bytes 491528 | tf_op jit(solution)/shard_map/ppermute | solution.py:23
  143.5 3.2 %collective-permute-start.37 = (bf16[32,1280]{1,0:T(8,128)(2,1)S(1)}, bf16[32,1280]{1,0:T(8,128)(2,1)S(1)}, u32[]{:S(2)}, u32[]{:S(2)}) collective-permute-start(bf16[32,1280]{1,0:T(8,128)(2,1)S(1)} %get-tuple-element.77), channel_id=1, source_target_pairs={{0,68},{32,100},{64,0},{96,32},{4,64},{36,96},{68,4},{100,36},{1,6... | collective-permute-start | bytes 245768 | tf_op jit(solution)/shard_map/ppermute | solution.py:23
  146.7 6.7 %shard_map.81 = f32[640,2560]{1,0:T(8,128)} custom-call(s32[4]{0:T(128)S(1)} %pad_add_fusion.s, bf16[256,2560]{1,0:T(8,128)(2,1)S(1)} %copy-done, bf16[256,2560]{1,0:T(8,128)(2,1)S(1)} %collective-permute-done.15.refs_4_.refs_1_, bf16[128,2560]{1,0:T(8,128)(2,1)S(1)} %collective-permute-done.4.refs_0_.refs_2_, ...), custom_call_target="tpu_custom_call" | custom-call | flops 3355443200 | bytes 13107200 | tf_op jit(solution)/shard_map/pallas_call | solution.py:129
  153.4 1.3 shard_map.79
  (42 shorter events, 0.3 us)
Async XLA Ops:
  0.6 5.8 %copy-start = (bf16[256,2560]{1,0:T(8,128)(2,1)S(1)}, bf16[256,2560]{1,0:T(8,128)(2,1)}, u32[]{:S(2)}) copy-start(bf16[256,2560]{1,0:T(8,128)(2,1)} %refs_0_.5) | copy-start | bytes 3932164
  2.2 19.3 %collective-permute-start = (bf16[128,2560]{1,0:T(8,128)(2,1)S(1)}, bf16[128,2560]{1,0:T(8,128)(2,1)S(1)}, u32[]{:S(2)}, u32[]{:S(2)}) collective-permute-start(bf16[128,2560]{1,0:T(8,128)(2,1)S(1)} %get-tuple-element.41), channel_id=1, source_target_pairs={{0,68},{32,100},{64,0},{96,32},{4,64},{36,96},{68,4},{100,36},{1,6... | collective-permute-start | bytes 1966088 | tf_op jit(solution)/shard_map/ppermute | solution.py:23
  6.4 32.4 %collective-permute-start.14 = (bf16[256,2560]{1,0:T(8,128)(2,1)}, bf16[256,2560]{1,0:T(8,128)(2,1)S(1)}, u32[]{:S(2)}, u32[]{:S(2)}) collective-permute-start(bf16[256,2560]{1,0:T(8,128)(2,1)} %refs_0_.4), channel_id=1, source_target_pairs={{0,32},{32,0},{64,96},{96,64},{4,36},{36,4},{68,100},{100,68},{1,3... | collective-permute-start | bytes 3932168 | tf_op jit(solution)/shard_map/ppermute | solution.py:23
  6.5 32.9 %collective-permute-start.15 = (bf16[256,2560]{1,0:T(8,128)(2,1)S(1)}, bf16[256,2560]{1,0:T(8,128)(2,1)S(1)}, u32[]{:S(2)}, u32[]{:S(2)}) collective-permute-start(bf16[256,2560]{1,0:T(8,128)(2,1)S(1)} %copy-done), channel_id=1, source_target_pairs={{0,32},{32,0},{64,96},{96,64},{4,36},{36,4},{68,100},{100,68},{1,3... | collective-permute-start | bytes 3932168 | tf_op jit(solution)/shard_map/ppermute | solution.py:23
  7.0 18.7 %collective-permute-start.1 = (bf16[128,2560]{1,0:T(8,128)(2,1)S(1)}, bf16[128,2560]{1,0:T(8,128)(2,1)S(1)}, u32[]{:S(2)}, u32[]{:S(2)}) collective-permute-start(bf16[128,2560]{1,0:T(8,128)(2,1)S(1)} %get-tuple-element.42), channel_id=1, source_target_pairs={{0,64},{32,96},{64,4},{96,36},{4,68},{36,100},{68,0},{100,32},{1,6... | collective-permute-start | bytes 1966088 | tf_op jit(solution)/shard_map/ppermute | solution.py:23
  7.6 26.9 %collective-permute-start.4 = (bf16[128,2560]{1,0:T(8,128)(2,1)S(1)}, bf16[128,2560]{1,0:T(8,128)(2,1)S(1)}, u32[]{:S(2)}, u32[]{:S(2)}) collective-permute-start(bf16[128,2560]{1,0:T(8,128)(2,1)S(1)} %get-tuple-element.44), channel_id=1, source_target_pairs={{0,68},{32,100},{64,0},{96,32},{4,64},{36,96},{68,4},{100,36},{1,6... | collective-permute-start | bytes 1966088 | tf_op jit(solution)/shard_map/ppermute | solution.py:23
  21.6 17.3 %collective-permute-start.5 = (bf16[128,2560]{1,0:T(8,128)(2,1)S(1)}, bf16[128,2560]{1,0:T(8,128)(2,1)S(1)}, u32[]{:S(2)}, u32[]{:S(2)}) collective-permute-start(bf16[128,2560]{1,0:T(8,128)(2,1)S(1)} %get-tuple-element.45), channel_id=1, source_target_pairs={{0,64},{32,96},{64,4},{96,36},{4,68},{36,100},{68,0},{100,32},{1,6... | collective-permute-start | bytes 1966088 | tf_op jit(solution)/shard_map/ppermute | solution.py:23
  25.7 25.0 %collective-permute-start.2 = (bf16[128,2560]{1,0:T(8,128)(2,1)S(1)}, bf16[128,2560]{1,0:T(8,128)(2,1)S(1)}, u32[]{:S(2)}, u32[]{:S(2)}) collective-permute-start(bf16[128,2560]{1,0:T(8,128)(2,1)S(1)} %collective-permute-done.refs_0_.refs_2_), channel_id=1, source_target_pairs={{0,32},{32,0},{64,96},{96,64},{4,36},{36,4},{68,100},{100,68},{1,3... | collective-permute-start | bytes 1966088 | tf_op jit(solution)/shard_map/ppermute | solution.py:23
  34.5 17.9 %collective-permute-start.3 = (bf16[128,2560]{1,0:T(8,128)(2,1)S(1)}, bf16[128,2560]{1,0:T(8,128)(2,1)S(1)}, u32[]{:S(2)}, u32[]{:S(2)}) collective-permute-start(bf16[128,2560]{1,0:T(8,128)(2,1)S(1)} %collective-permute-done.1.refs_1_.refs_3_), channel_id=1, source_target_pairs={{0,32},{32,0},{64,96},{96,64},{4,36},{36,4},{68,100},{100,68},{1,3... | collective-permute-start | bytes 1966088 | tf_op jit(solution)/shard_map/ppermute | solution.py:23
  38.9 18.2 %collective-permute-start.6 = (bf16[128,2560]{1,0:T(8,128)(2,1)S(1)}, bf16[128,2560]{1,0:T(8,128)(2,1)S(1)}, u32[]{:S(2)}, u32[]{:S(2)}) collective-permute-start(bf16[128,2560]{1,0:T(8,128)(2,1)S(1)} %collective-permute-done.4.refs_0_.refs_2_), channel_id=1, source_target_pairs={{0,32},{32,0},{64,96},{96,64},{4,36},{36,4},{68,100},{100,68},{1,3... | collective-permute-start | bytes 1966088 | tf_op jit(solution)/shard_map/ppermute | solution.py:23
  38.9 18.9 %collective-permute-start.7 = (bf16[128,2560]{1,0:T(8,128)(2,1)S(1)}, bf16[128,2560]{1,0:T(8,128)(2,1)S(1)}, u32[]{:S(2)}, u32[]{:S(2)}) collective-permute-start(bf16[128,2560]{1,0:T(8,128)(2,1)S(1)} %collective-permute-done.5.refs_1_.refs_3_), channel_id=1, source_target_pairs={{0,32},{32,0},{64,96},{96,64},{4,36},{36,4},{68,100},{100,68},{1,3... | collective-permute-start | bytes 1966088 | tf_op jit(solution)/shard_map/ppermute | solution.py:23
  39.4 1.9 %copy-start.1 = (bf16[640,2560]{1,0:T(8,128)(2,1)S(1)}, bf16[640,2560]{1,0:T(8,128)(2,1)}, u32[]{:S(2)}) copy-start(bf16[640,2560]{1,0:T(8,128)(2,1)} %refs_5_.1) | copy-start | bytes 9830404
  41.3 1.9 %copy-start.2 = (bf16[2560,640]{1,0:T(8,128)(2,1)S(1)}, bf16[2560,640]{1,0:T(8,128)(2,1)}, u32[]{:S(2)}) copy-start(bf16[2560,640]{1,0:T(8,128)(2,1)} %w_ref.3) | copy-start | bytes 9830404
  49.0 23.3 %collective-permute-start.16 = (bf16[2,2,64,640]{3,2,1,0:T(8,128)(2,1)S(1)}, bf16[2,2,64,640]{3,2,1,0:T(8,128)(2,1)S(1)}, u32[]{:S(2)}, u32[]{:S(2)}) collective-permute-start(bf16[2,2,64,640]{3,2,1,0:T(8,128)(2,1)S(1)} %get-tuple-element.54), channel_id=1, source_target_pairs={{0,8},{32,40},{64,72},{96,104},{4,12},{36,44},{68,76},{100,108},{1... | collective-permute-start | bytes 983048 | tf_op jit(solution)/shard_map/ppermute | solution.py:23
  50.6 22.3 %collective-permute-start.17 = (bf16[2,2,64,640]{3,2,1,0:T(8,128)(2,1)S(1)}, bf16[2,2,64,640]{3,2,1,0:T(8,128)(2,1)S(1)}, u32[]{:S(2)}, u32[]{:S(2)}) collective-permute-start(bf16[2,2,64,640]{3,2,1,0:T(8,128)(2,1)S(1)} %get-tuple-element.55), channel_id=1, source_target_pairs={{0,24},{32,56},{64,88},{96,120},{4,28},{36,60},{68,92},{100,124},{... | collective-permute-start | bytes 983048 | tf_op jit(solution)/shard_map/ppermute | solution.py:23
  52.4 23.2 %collective-permute-start.18 = (bf16[2,2,64,640]{3,2,1,0:T(8,128)(2,1)S(1)}, bf16[2,2,64,640]{3,2,1,0:T(8,128)(2,1)S(1)}, u32[]{:S(2)}, u32[]{:S(2)}) collective-permute-start(bf16[2,2,64,640]{3,2,1,0:T(8,128)(2,1)S(1)} %get-tuple-element.56), channel_id=1, source_target_pairs={{0,16},{32,48},{64,80},{96,112},{4,20},{36,52},{68,84},{100,116},{... | collective-permute-start | bytes 983048 | tf_op jit(solution)/shard_map/ppermute | solution.py:23
  57.0 13.5 %collective-permute-start.8 = (bf16[1,2,64,640]{3,2,1,0:T(8,128)(2,1)S(1)}, bf16[1,2,64,640]{3,2,1,0:T(8,128)(2,1)S(1)}, u32[]{:S(2)}, u32[]{:S(2)}) collective-permute-start(bf16[1,2,64,640]{3,2,1,0:T(8,128)(2,1)S(1)} %get-tuple-element.47), channel_id=1, source_target_pairs={{0,8},{32,40},{64,72},{96,104},{4,12},{36,44},{68,76},{100,108},{1... | collective-permute-start | bytes 491528 | tf_op jit(solution)/shard_map/ppermute | solution.py:23
  57.7 19.2 %collective-permute-start.9 = (bf16[1,2,64,640]{3,2,1,0:T(8,128)(2,1)S(1)}, bf16[1,2,64,640]{3,2,1,0:T(8,128)(2,1)S(1)}, u32[]{:S(2)}, u32[]{:S(2)}) collective-permute-start(bf16[1,2,64,640]{3,2,1,0:T(8,128)(2,1)S(1)} %get-tuple-element.48), channel_id=1, source_target_pairs={{0,24},{32,56},{64,88},{96,120},{4,28},{36,60},{68,92},{100,124},{... | collective-permute-start | bytes 491528 | tf_op jit(solution)/shard_map/ppermute | solution.py:23
  70.6 8.6 %collective-permute-start.10 = (bf16[1,2,64,640]{3,2,1,0:T(8,128)(2,1)S(1)}, bf16[1,2,64,640]{3,2,1,0:T(8,128)(2,1)S(1)}, u32[]{:S(2)}, u32[]{:S(2)}) collective-permute-start(bf16[1,2,64,640]{3,2,1,0:T(8,128)(2,1)S(1)} %get-tuple-element.49), channel_id=1, source_target_pairs={{0,16},{32,48},{64,80},{96,112},{4,20},{36,52},{68,84},{100,116},{... | collective-permute-start | bytes 491528 | tf_op jit(solution)/shard_map/ppermute | solution.py:23
  72.3 11.8 %collective-permute-start.11 = (bf16[1,2,64,640]{3,2,1,0:T(8,128)(2,1)S(1)}, bf16[1,2,64,640]{3,2,1,0:T(8,128)(2,1)S(1)}, u32[]{:S(2)}, u32[]{:S(2)}) collective-permute-start(bf16[1,2,64,640]{3,2,1,0:T(8,128)(2,1)S(1)} %get-tuple-element.50), channel_id=1, source_target_pairs={{0,8},{32,40},{64,72},{96,104},{4,12},{36,44},{68,76},{100,108},{1... | collective-permute-start | bytes 491528 | tf_op jit(solution)/shard_map/ppermute | solution.py:23
  72.9 12.3 %collective-permute-start.12 = (bf16[1,2,64,640]{3,2,1,0:T(8,128)(2,1)S(1)}, bf16[1,2,64,640]{3,2,1,0:T(8,128)(2,1)S(1)}, u32[]{:S(2)}, u32[]{:S(2)}) collective-permute-start(bf16[1,2,64,640]{3,2,1,0:T(8,128)(2,1)S(1)} %get-tuple-element.51), channel_id=1, source_target_pairs={{0,24},{32,56},{64,88},{96,120},{4,28},{36,60},{68,92},{100,124},{... | collective-permute-start | bytes 491528 | tf_op jit(solution)/shard_map/ppermute | solution.py:23
  75.5 10.6 %collective-permute-start.13 = (bf16[1,2,64,640]{3,2,1,0:T(8,128)(2,1)S(1)}, bf16[1,2,64,640]{3,2,1,0:T(8,128)(2,1)S(1)}, u32[]{:S(2)}, u32[]{:S(2)}) collective-permute-start(bf16[1,2,64,640]{3,2,1,0:T(8,128)(2,1)S(1)} %get-tuple-element.52), channel_id=1, source_target_pairs={{0,16},{32,48},{64,80},{96,112},{4,20},{36,52},{68,84},{100,116},{... | collective-permute-start | bytes 491528 | tf_op jit(solution)/shard_map/ppermute | solution.py:23
  76.1 17.1 %copy-start.3 = (bf16[2560,640]{1,0:T(8,128)(2,1)S(1)}, bf16[2560,640]{1,0:T(8,128)(2,1)}, u32[]{:S(2)}) copy-start(bf16[2560,640]{1,0:T(8,128)(2,1)} %w_ref.3) | copy-start | bytes 9830404
  77.0 14.8 %collective-permute-start.28 = (bf16[2,64,640]{2,1,0:T(8,128)(2,1)S(1)}, bf16[2,64,640]{2,1,0:T(8,128)(2,1)S(1)}, u32[]{:S(2)}, u32[]{:S(2)}) collective-permute-start(bf16[2,64,640]{2,1,0:T(8,128)(2,1)S(1)} %get-tuple-element.67.p0.refs_6_), channel_id=1, source_target_pairs={{0,8},{32,40},{64,72},{96,104},{4,12},{36,44},{68,76},{100,108},{1... | collective-permute-start | bytes 491528 | tf_op jit(solution)/shard_map/ppermute | solution.py:23
  79.1 14.0 %collective-permute-start.29 = (bf16[2,64,640]{2,1,0:T(8,128)(2,1)S(1)}, bf16[2,64,640]{2,1,0:T(8,128)(2,1)S(1)}, u32[]{:S(2)}, u32[]{:S(2)}) collective-permute-start(bf16[2,64,640]{2,1,0:T(8,128)(2,1)S(1)} %get-tuple-element.67.p0.refs_6_), channel_id=1, source_target_pairs={{0,16},{32,48},{64,80},{96,112},{4,20},{36,52},{68,84},{100,116},{... | collective-permute-start | bytes 491528 | tf_op jit(solution)/shard_map/ppermute | solution.py:23
  84.1 9.1 %collective-permute-start.30 = (bf16[2,64,640]{2,1,0:T(8,128)(2,1)S(1)}, bf16[2,64,640]{2,1,0:T(8,128)(2,1)S(1)}, u32[]{:S(2)}, u32[]{:S(2)}) collective-permute-start(bf16[2,64,640]{2,1,0:T(8,128)(2,1)S(1)} %get-tuple-element.67.p0.refs_6_), channel_id=1, source_target_pairs={{0,24},{32,56},{64,88},{96,120},{4,28},{36,60},{68,92},{100,124},{... | collective-permute-start | bytes 491528 | tf_op jit(solution)/shard_map/ppermute | solution.py:23
  87.0 9.7 %collective-permute-start.19 = (bf16[2,64,640]{2,1,0:T(8,128)(2,1)S(1)}, bf16[2,64,640]{2,1,0:T(8,128)(2,1)S(1)}, u32[]{:S(2)}, u32[]{:S(2)}) collective-permute-start(bf16[2,64,640]{2,1,0:T(8,128)(2,1)S(1)} %get-tuple-element.58.p0.refs_10_), channel_id=1, source_target_pairs={{0,8},{32,40},{64,72},{96,104},{4,12},{36,44},{68,76},{100,108},{1... | collective-permute-start | bytes 491528 | tf_op jit(solution)/shard_map/ppermute | solution.py:23
  87.3 11.1 %collective-permute-start.20 = (bf16[2,64,640]{2,1,0:T(8,128)(2,1)S(1)}, bf16[2,64,640]{2,1,0:T(8,128)(2,1)S(1)}, u32[]{:S(2)}, u32[]{:S(2)}) collective-permute-start(bf16[2,64,640]{2,1,0:T(8,128)(2,1)S(1)} %get-tuple-element.58.p0.refs_10_), channel_id=1, source_target_pairs={{0,16},{32,48},{64,80},{96,112},{4,20},{36,52},{68,84},{100,116},{... | collective-permute-start | bytes 491528 | tf_op jit(solution)/shard_map/ppermute | solution.py:23
  91.8 6.6 %collective-permute-start.21 = (bf16[2,64,640]{2,1,0:T(8,128)(2,1)S(1)}, bf16[2,64,640]{2,1,0:T(8,128)(2,1)S(1)}, u32[]{:S(2)}, u32[]{:S(2)}) collective-permute-start(bf16[2,64,640]{2,1,0:T(8,128)(2,1)S(1)} %get-tuple-element.58.p0.refs_10_), channel_id=1, source_target_pairs={{0,24},{32,56},{64,88},{96,120},{4,28},{36,60},{68,92},{100,124},{... | collective-permute-start | bytes 491528 | tf_op jit(solution)/shard_map/ppermute | solution.py:23
  96.0 5.4 %collective-permute-start.31 = (bf16[256,2560]{1,0:T(8,128)(2,1)S(1)}, bf16[256,2560]{1,0:T(8,128)(2,1)S(1)}, u32[]{:S(2)}, u32[]{:S(2)}) collective-permute-start(bf16[256,2560]{1,0:T(8,128)(2,1)S(1)} %get-tuple-element.69), channel_id=1, source_target_pairs={{0,32},{32,0},{64,96},{96,64},{4,36},{36,4},{68,100},{100,68},{1,3... | collective-permute-start | bytes 3932168 | tf_op jit(solution)/shard_map/ppermute | solution.py:23
  101.2 3.1 %collective-permute-start.22 = (bf16[256,2560]{1,0:T(8,128)(2,1)S(1)}, bf16[256,2560]{1,0:T(8,128)(2,1)S(1)}, u32[]{:S(2)}, u32[]{:S(2)}) collective-permute-start(bf16[256,2560]{1,0:T(8,128)(2,1)S(1)} %get-tuple-element.60), channel_id=1, source_target_pairs={{0,32},{32,0},{64,96},{96,64},{4,36},{36,4},{68,100},{100,68},{1,3... | collective-permute-start | bytes 3932168 | tf_op jit(solution)/shard_map/ppermute | solution.py:23
  102.1 35.2 %collective-permute-start.32 = (bf16[128,2560]{1,0:T(8,128)(2,1)S(1)}, bf16[128,2560]{1,0:T(8,128)(2,1)S(1)}, u32[]{:S(2)}, u32[]{:S(2)}) collective-permute-start(bf16[128,2560]{1,0:T(8,128)(2,1)S(1)} %get-tuple-element.71), channel_id=1, source_target_pairs={{0,4},{32,36},{64,68},{96,100},{4,0},{36,32},{68,64},{100,96},{1,5... | collective-permute-start | bytes 1966088 | tf_op jit(solution)/shard_map/ppermute | solution.py:23
  105.1 22.7 %collective-permute-start.26 = (bf16[128,1280]{1,0:T(8,128)(2,1)S(1)}, bf16[128,1280]{1,0:T(8,128)(2,1)S(1)}, u32[]{:S(2)}, u32[]{:S(2)}) collective-permute-start(bf16[128,1280]{1,0:T(8,128)(2,1)S(1)} %get-tuple-element.65), channel_id=1, source_target_pairs={{0,64},{32,96},{64,4},{96,36},{4,68},{36,100},{68,0},{100,32},{1,6... | collective-permute-start | bytes 983048 | tf_op jit(solution)/shard_map/ppermute | solution.py:23
  105.2 7.6 %collective-permute-start.23 = (bf16[2,32,1280]{2,1,0:T(8,128)(2,1)S(1)}, bf16[2,32,1280]{2,1,0:T(8,128)(2,1)S(1)}, u32[]{:S(2)}, u32[]{:S(2)}) collective-permute-start(bf16[2,32,1280]{2,1,0:T(8,128)(2,1)S(1)} %get-tuple-element.62), channel_id=1, source_target_pairs={{0,1},{32,33},{64,65},{96,97},{4,5},{36,37},{68,69},{100,101},{1,2... | collective-permute-start | bytes 491528 | tf_op jit(solution)/shard_map/ppermute | solution.py:23
  106.8 8.8 %collective-permute-start.24 = (bf16[2,32,1280]{2,1,0:T(8,128)(2,1)S(1)}, bf16[2,32,1280]{2,1,0:T(8,128)(2,1)S(1)}, u32[]{:S(2)}, u32[]{:S(2)}) collective-permute-start(bf16[2,32,1280]{2,1,0:T(8,128)(2,1)S(1)} %get-tuple-element.63), channel_id=1, source_target_pairs={{0,3},{32,35},{64,67},{96,99},{4,7},{36,39},{68,71},{100,103},{1,0... | collective-permute-start | bytes 491528 | tf_op jit(solution)/shard_map/ppermute | solution.py:23
  108.5 9.0 %collective-permute-start.25 = (bf16[2,32,1280]{2,1,0:T(8,128)(2,1)S(1)}, bf16[2,32,1280]{2,1,0:T(8,128)(2,1)S(1)}, u32[]{:S(2)}, u32[]{:S(2)}) collective-permute-start(bf16[2,32,1280]{2,1,0:T(8,128)(2,1)S(1)} %get-tuple-element.64), channel_id=1, source_target_pairs={{0,2},{32,34},{64,66},{96,98},{4,6},{36,38},{68,70},{100,102},{1,3... | collective-permute-start | bytes 491528 | tf_op jit(solution)/shard_map/ppermute | solution.py:23
  112.8 24.5 %collective-permute-start.27 = (bf16[128,1280]{1,0:T(8,128)(2,1)S(1)}, bf16[128,1280]{1,0:T(8,128)(2,1)S(1)}, u32[]{:S(2)}, u32[]{:S(2)}) collective-permute-start(bf16[128,1280]{1,0:T(8,128)(2,1)S(1)} %get-tuple-element.66), channel_id=1, source_target_pairs={{0,68},{32,100},{64,0},{96,32},{4,64},{36,96},{68,4},{100,36},{1,6... | collective-permute-start | bytes 983048 | tf_op jit(solution)/shard_map/ppermute | solution.py:23
  115.7 25.8 %collective-permute-start.38 = (bf16[2,2,64,640]{3,2,1,0:T(8,128)(2,1)S(1)}, bf16[2,2,64,640]{3,2,1,0:T(8,128)(2,1)S(1)}, u32[]{:S(2)}, u32[]{:S(2)}) collective-permute-start(bf16[2,2,64,640]{3,2,1,0:T(8,128)(2,1)S(1)} %get-tuple-element.78.refs_6_), channel_id=1, source_target_pairs={{0,8},{32,40},{64,72},{96,104},{4,12},{36,44},{68,76},{100,108},{1... | collective-permute-start | bytes 983048 | tf_op jit(solution)/shard_map/ppermute | solution.py:23
  117.5 26.0 %collective-permute-start.39 = (bf16[2,2,64,640]{3,2,1,0:T(8,128)(2,1)S(1)}, bf16[2,2,64,640]{3,2,1,0:T(8,128)(2,1)S(1)}, u32[]{:S(2)}, u32[]{:S(2)}) collective-permute-start(bf16[2,2,64,640]{3,2,1,0:T(8,128)(2,1)S(1)} %get-tuple-element.78.refs_6_), channel_id=1, source_target_pairs={{0,16},{32,48},{64,80},{96,112},{4,20},{36,52},{68,84},{100,116},{... | collective-permute-start | bytes 983048 | tf_op jit(solution)/shard_map/ppermute | solution.py:23
  127.9 15.6 %collective-permute-start.40 = (bf16[2,2,64,640]{3,2,1,0:T(8,128)(2,1)S(1)}, bf16[2,2,64,640]{3,2,1,0:T(8,128)(2,1)S(1)}, u32[]{:S(2)}, u32[]{:S(2)}) collective-permute-start(bf16[2,2,64,640]{3,2,1,0:T(8,128)(2,1)S(1)} %get-tuple-element.78.refs_6_), channel_id=1, source_target_pairs={{0,24},{32,56},{64,88},{96,120},{4,28},{36,60},{68,92},{100,124},{... | collective-permute-start | bytes 983048 | tf_op jit(solution)/shard_map/ppermute | solution.py:23
  138.2 15.2 %collective-permute-start.33 = (bf16[32,2560]{1,0:T(8,128)(2,1)S(1)}, bf16[32,2560]{1,0:T(8,128)(2,1)S(1)}, u32[]{:S(2)}, u32[]{:S(2)}) collective-permute-start(bf16[32,2560]{1,0:T(8,128)(2,1)S(1)} %get-tuple-element.73), channel_id=1, source_target_pairs={{0,1},{32,33},{64,65},{96,97},{4,5},{36,37},{68,69},{100,101},{1,2... | collective-permute-start | bytes 491528 | tf_op jit(solution)/shard_map/ppermute | solution.py:23
  139.8 13.6 %collective-permute-start.34 = (bf16[32,2560]{1,0:T(8,128)(2,1)S(1)}, bf16[32,2560]{1,0:T(8,128)(2,1)S(1)}, u32[]{:S(2)}, u32[]{:S(2)}) collective-permute-start(bf16[32,2560]{1,0:T(8,128)(2,1)S(1)} %get-tuple-element.74), channel_id=1, source_target_pairs={{0,3},{32,35},{64,67},{96,99},{4,7},{36,39},{68,71},{100,103},{1,0... | collective-permute-start | bytes 491528 | tf_op jit(solution)/shard_map/ppermute | solution.py:23
  141.5 11.9 %collective-permute-start.35 = (bf16[32,2560]{1,0:T(8,128)(2,1)S(1)}, bf16[32,2560]{1,0:T(8,128)(2,1)S(1)}, u32[]{:S(2)}, u32[]{:S(2)}) collective-permute-start(bf16[32,2560]{1,0:T(8,128)(2,1)S(1)} %get-tuple-element.75), channel_id=1, source_target_pairs={{0,2},{32,34},{64,66},{96,98},{4,6},{36,38},{68,70},{100,102},{1,3... | collective-permute-start | bytes 491528 | tf_op jit(solution)/shard_map/ppermute | solution.py:23
  143.5 9.9 %collective-permute-start.36 = (bf16[32,1280]{1,0:T(8,128)(2,1)S(1)}, bf16[32,1280]{1,0:T(8,128)(2,1)S(1)}, u32[]{:S(2)}, u32[]{:S(2)}) collective-permute-start(bf16[32,1280]{1,0:T(8,128)(2,1)S(1)} %get-tuple-element.76), channel_id=1, source_target_pairs={{0,64},{32,96},{64,4},{96,36},{4,68},{36,100},{68,0},{100,32},{1,6... | collective-permute-start | bytes 245768 | tf_op jit(solution)/shard_map/ppermute | solution.py:23
  143.5 9.9 %collective-permute-start.37 = (bf16[32,1280]{1,0:T(8,128)(2,1)S(1)}, bf16[32,1280]{1,0:T(8,128)(2,1)S(1)}, u32[]{:S(2)}, u32[]{:S(2)}) collective-permute-start(bf16[32,1280]{1,0:T(8,128)(2,1)S(1)} %get-tuple-element.77), channel_id=1, source_target_pairs={{0,68},{32,100},{64,0},{96,32},{4,64},{36,96},{68,4},{100,36},{1,6... | collective-permute-start | bytes 245768 | tf_op jit(solution)/shard_map/ppermute | solution.py:23

commit v2 on v1

--- a/solution.py
+++ b/solution.py
@@ -6,6 +6,8 @@
 from jax.sharding import PartitionSpec as P
 
 INTERPRET = False
+WARM = 30_000_000_000
+FIRST_TILE, SECOND_TILE = 1280, 1280
 AXES = ("tok", "con", "out")
 BF, F32 = jnp.bfloat16, jnp.float32
 
@@ -14,10 +16,10 @@
     return (((z % 2) * 2 + k) * 4 + x) * 8 + (z // 2) * 4 + y
 
 
-def shift(v, x=0, y=0, z=0, k=0):
+def shift(v, x=0, y=0, z=(0, 0), k=0):
     r = range(4)
     pairs = [
-        (index_of(a, b, c, d), index_of((a + x) % 4, (b + y) % 4, (c + z) % 4, (d + k) % 2))
+        (index_of(a, b, c, d), index_of((a + x) % 4, (b + y) % 4, (c + z[d]) % 4, (d + k) % 2))
         for a in r for b in r for c in r for d in range(2)
     ]
     return lax.ppermute(v, AXES, pairs)
@@ -84,31 +86,70 @@
     return sent, keep
 
 
-def back(scal, parts, pick, w):
+def warm(scal):
+    def body(s, o):
+        for i in range(scal.shape[0]):
+            o[i] = s[i]
+
+    smem = pl.BlockSpec(memory_space=pltpu.SMEM)
+    return pl.pallas_call(
+        body,
+        in_specs=[smem],
+        out_specs=smem,
+        out_shape=jax.ShapeDtypeStruct(scal.shape, scal.dtype),
+        cost_estimate=pl.CostEstimate(flops=WARM, bytes_accessed=32, transcendentals=0),
+        compiler_params=pltpu.CompilerParams(vmem_limit_bytes=1 << 20),
+        interpret=INTERPRET,
+    )(scal)
+
+
+def project_block(scal, rows, w, dim, prior=None):
+    hidden = w.shape[1 - dim]
+    quarter = rows.shape[0] // 4
+    last = prior is not None
+
+    def body(s, v, w, *refs):
+        outs, part = refs[-5:-1], refs[-1]
+        part[...] = product(v[...], w[...], 1, dim)
+        for i, (o, j) in enumerate(zip(outs, (1, 3, 2, 0))):
+            new = part[pl.ds(lax.rem(s[0] + j, 4) * quarter, quarter), :].astype(o.dtype)
+            if last:
+                o[0, 0] = refs[i][...]
+                o[0, 1] = new
+            else:
+                o[...] = new
+
+    shape = (1, 2, quarter, hidden) if last else (quarter, hidden)
+    return run(
+        body, [(shape, BF)] * 3 + [(shape, F32)], scal, [rows, w, *(prior or [])],
+        [pltpu.VMEM((4 * quarter, hidden), F32)], 2 * rows.shape[0] * w.size, 6 << 20)
+
+
+def back(scal, parts, b, w, kind):
     width = w.shape[0]
     quarter, hidden = parts[0].shape[-2:]
     tile = 512 if width % 512 == 0 else 128
 
-    def body(s, p0, p1, p2, p3, w_ref, other, mine):
-        x = s[0]
-        lhs = jnp.concatenate([pick(p)[b] for b in range(2) for p in (p0, p1, p2, p3)], axis=0)
+    def body(s, p0, p1, p2, p3, w_ref, out):
+        lhs = jnp.concatenate([p[b] for p in (p0, p1, p2, p3)], axis=0)
         for t in range(0, width, tile):
             res = product(lhs, w_ref[t : t + tile, :], 1, 1)
             for j in range(4):
-                at = pl.ds(lax.rem(x + 4 - j, 4) * quarter, quarter)
-                mine[at, t : t + tile] = res[j * quarter : (j + 1) * quarter]
-                other[at, t : t + tile] = res[(4 + j) * quarter : (5 + j) * quarter].astype(BF)
-
-    return run(
-        body, [((4 * quarter, width), BF), ((4 * quarter, width), F32)], scal, [*parts, w],
-        flops=16 * quarter * hidden * width, room=8 << 20)
+                at = pl.ds(lax.rem(s[0] + 4 - j, 4) * quarter, quarter)
+                out[at, t : t + tile] = res[j * quarter : (j + 1) * quarter].astype(kind)
+
+    (out,) = run(
+        body, [((4 * quarter, width), kind)], scal, [*parts, w],
+        flops=8 * quarter * hidden * width, room=6 << 20)
+    return out
 
 
 def weight_grad(scal, lefts, rights, pick, tile_left):
     blocks, parts = (lefts, rights) if tile_left else (rights, lefts)
     width = blocks[0].shape[1]
     quarter, hidden = parts[0].shape[-2:]
-    tile = 512 if width % 512 == 0 else 128
+    wanted = FIRST_TILE if tile_left else SECOND_TILE
+    tile = wanted if width % wanted == 0 else 128
     rows = sum(v.shape[0] for v in blocks)
 
     def body(s, *refs):
@@ -138,7 +179,7 @@
         cost_estimate=pl.CostEstimate(
             flops=2 * rows * width * hidden, bytes_accessed=2 * rows * (width + hidden) + 4 * width * hidden,
             transcendentals=0),
-        compiler_params=pltpu.CompilerParams(vmem_limit_bytes=20 << 20),
+        compiler_params=pltpu.CompilerParams(vmem_limit_bytes=30 << 20),
         interpret=INTERPRET,
     )(scal, *blocks, *parts)
 
@@ -167,24 +208,14 @@
     return run(body, [((2,) * len(more) + shape, BF), (shape, BF)], scal, [*own, *got, *more])
 
 
-def cut(scal, v):
-    n = v.shape[0] // 2
-
-    def body(s, v, a, b):
-        a[...] = v[:n]
-        b[...] = v[n:]
-
-    return run(body, [((n, v.shape[1]), BF)] * 2, scal, [v], room=1 << 20)
-
-
 def body_of(tokens, out_grad, weight_in, weight_out):
     ix = lax.axis_index("con")
     it, io = lax.axis_index("tok"), lax.axis_index("out")
     zl, zh, iy = it >> 1, io >> 2, io & 3
     scal = jnp.stack([ix, iy, zh, zh ^ zl]).astype(jnp.int32)
+    scal = warm(scal)
     rows, width = tokens.shape
     half, small = width // 2, rows // 8
-    whole = lambda v: v[...]
 
     def around(sent, name):
         return [shift(v, **{name: j}) for v, j in zip(sent, (1, 3, 2))]
@@ -192,26 +223,27 @@
     def spread(v):
         return [v] + [shift(v, x=j) for j in (1, 2, 3)]
 
-    partner, top = [], []
+    partner, far = [], []
     for v in (tokens, out_grad):
         partner.append(shift(v, k=1))
-        up, down = cut(scal, v)
-        top.append([shift(up, z=3), shift(down, z=1)])
+        far.append(shift(v, z=(3, 1)))
     sent_l, keep_l = project(
         scal, [((tokens, partner[0]), weight_in, 0), ((out_grad, partner[1]), weight_out, 1)])
     got_l = around(sent_l, "x")
-    far_t = top[0] + [shift(v, k=1) for v in top[0]]
-    sent_r, keep_r = project(scal, [(far_t, weight_in, 0)])
+    far_t = [far[0], shift(far[0], k=1)]
+    prior = project_block(scal, far_t[0], weight_in, 0)
+    *sent_r, keep_r = project_block(scal, far_t[1], weight_in, 0, prior)
     got_r = around(sent_r, "x")
     ac_l, pg_l = gelu(scal, [keep_l], got_l, ((0, 0), (0, 1)))
     pg_l = spread(pg_l)
 
-    far_g = top[1] + [shift(v, k=1) for v in top[1]]
-    sent_g, keep_g = project(scal, [(far_g, weight_out, 1)])
+    far_g = [far[1], shift(far[1], k=1)]
+    prior = project_block(scal, far_g[0], weight_out, 1)
+    *sent_g, keep_g = project_block(scal, far_g[1], weight_out, 1, prior)
     got_g = around(sent_g, "x")
 
-    other_l, mine_l = back(scal, pg_l, whole, weight_in)
-    swapped_l = shift(other_l, k=1)
+    swapped_l = shift(back(scal, pg_l, 1, weight_in, BF), k=1)
+    mine_l = back(scal, pg_l, 0, weight_in, F32)
     activ_q, pre_grad_q = gelu(scal, [keep_r, keep_g], [*got_r, *got_g], ((0, 0), (1, 0)), ac_l)
     pg_r = spread(pre_grad_q)
     activ = spread(activ_q)
@@ -224,10 +256,10 @@
 
     send, keep = run(
         mid_l, [((4 * small, width), BF), ((4 * small, width), F32)], scal, [mine_l, swapped_l])
-    other = shift(send, z=2)
-
-    other_r, mine_r = back(scal, pg_r, whole, weight_in)
-    swapped_r = shift(other_r, k=1)
+    other = shift(send, z=(2, 2))
+
+    swapped_r = shift(back(scal, pg_r, 1, weight_in, BF), k=1)
+    mine_r = back(scal, pg_r, 0, weight_in, F32)
 
     def mid_r(s, mine, got, o1, o3, o2, stay, up, down):
         for g in range(2):
@@ -245,7 +277,7 @@
     *send, stay, up, down = run(
         mid_r, [(group, BF)] * 3 + [(group, F32)] + [(part, BF)] * 2, scal, [mine_r, swapped_r])
     got_a = around(send, "y")
-    got_b = [shift(up, z=1), shift(down, z=3)]
+    got_b = [shift(up, z=(1, 1)), shift(down, z=(3, 3))]
     first_grad = weight_grad(
         scal, [tokens, partner[0], *far_t], [*pg_l, *pg_r], lambda v, c, j: v[4 * c + j], True)
 
@@ -261,7 +293,7 @@
     up, down, *send, own = run(
         next_r, [((small, half), BF)] * 2 + [((small, width), BF)] * 3 + [((small, width), F32)], scal,
         [stay, *got_a, *got_b, keep, other])
-    got_a = [shift(up, z=1), shift(down, z=3)]
+    got_a = [shift(up, z=(1, 1)), shift(down, z=(3, 3))]
     got_b = around(send, "y")
     second_grad = weight_grad(
         scal, activ, [out_grad, partner[1], *far_g], lambda v, c, j: v[j].at[c], False)

time: 155 us -> 162 us (1.045)
  the two profiles are of different devices: /device:TPU:0 before, /device:TPU:26 now
where the time goes in v2:
time: 162 us; the launch traced here: 160 us
  waiting for transfers between devices  66.7 us (41%)
  starting transfers between devices  50.8 us (31%)
  Pallas kernels  41.2 us (25%)
    ppermute x37, waiting for transfers between devices, shift(): return lax.ppermute(v, AXES, pairs)  66.7 us
    ppermute x37, starting transfers between devices, shift(): return lax.ppermute(v, AXES, pairs)  50.8 us
    pallas_call x15, Pallas kernels, run(): pl.pallas_call(body, in_specs=[pl.BlockSpec(memory_space=pltpu.SMEM)] + [...  25.8 us
    pallas_call x2, Pallas kernels, weight_grad(): pl.pallas_call(body, grid=(width // tile,), in_specs=[pl.BlockSpec(memory...  14.3 us
  transfers between devices with their start and end apart: 37, of which 15 were waited for; matrix products, arithmetic and copies ran while one was open for 0% of the time, Pallas kernels for 25%

profile of v2, /device:TPU:26, one launch (start us, length us, event | category | flops | bytes accessed | tf_op | source)
XLA Modules:
  0.0 159.8 jit_solution(8721540475088441553)
XLA Ops:
  0.6 4.1 %collective-permute-start = (bf16[256,2560]{1,0:T(8,128)(2,1)}, bf16[256,2560]{1,0:T(8,128)(2,1)S(1)}, u32[]{:S(2)}, u32[]{:S(2)}) collective-permute-start(bf16[256,2560]{1,0:T(8,128)(2,1)} %refs_0_.4), channel_id=1, source_target_pairs={{0,68},{32,96},{64,0},{96,36},{4,64},{36,100},{68,4},{100,32},{1,6... | collective-permute-start | bytes 3932168 | tf_op jit(solution)/shard_map/ppermute | solution.py:25
  4.7 0.4 collective-permute-start.2
  5.1 0.5 collective-permute-start.11
  5.7 14.4 %collective-permute-done.v.refs_2_ = bf16[256,2560]{1,0:T(8,128)(2,1)S(1)} collective-permute-done((bf16[256,2560]{1,0:T(8,128)(2,1)}, bf16[256,2560]{1,0:T(8,128)(2,1)S(1)}, u32[]{:S(2)}, u32[]{:S(2)}) %collective-permute-start) | collective-permute-done | bytes 1310752 | tf_op jit(solution)/shard_map/ppermute | solution.py:25
  20.2 14.0 %collective-permute-done.2.v.refs_2_ = bf16[256,2560]{1,0:T(8,128)(2,1)S(1)} collective-permute-done((bf16[256,2560]{1,0:T(8,128)(2,1)}, bf16[256,2560]{1,0:T(8,128)(2,1)S(1)}, u32[]{:S(2)}, u32[]{:S(2)}) %collective-permute-start.2) | collective-permute-done | bytes 1310752 | tf_op jit(solution)/shard_map/ppermute | solution.py:25
  34.2 1.1 shard_map.67.s
  35.4 6.2 %shard_map.72 = (bf16[2,2,64,640]{3,2,1,0:T(8,128)(2,1)S(1)}, bf16[2,2,64,640]{3,2,1,0:T(8,128)(2,1)S(1)}, bf16[2,2,64,640]{3,2,1,0:T(8,128)(2,1)S(1)}, f32[2,2,64,640]{3,2,1,0:T(8,128)S(1)}) custom-call(s32[4]{0:T(128)S(1)} %shard_map.67.s, bf16[256,2560]{1,0:T(8,128)(2,1)S(1)} %copy-done.2, bf16[256,2560]{1,0:T(8,128)(2,1)} %collective-permute-done.10.refs_1_, ...), custom_call_target="tpu_custom_call" | custom-call | flops 3355443200 | bytes 13434880 | tf_op jit(solution)/shard_map/pallas_call | solution.py:40
  41.7 1.6 collective-permute-start.12
  43.2 0.5 collective-permute-start.13
  43.7 2.1 %collective-permute-start.14 = (bf16[2,2,64,640]{3,2,1,0:T(8,128)(2,1)S(1)}, bf16[2,2,64,640]{3,2,1,0:T(8,128)(2,1)S(1)}, u32[]{:S(2)}, u32[]{:S(2)}) collective-permute-start(bf16[2,2,64,640]{3,2,1,0:T(8,128)(2,1)S(1)} %get-tuple-element.60), channel_id=1, source_target_pairs={{0,16},{32,48},{64,80},{96,112},{4,20},{36,52},{68,84},{100,116},{... | collective-permute-start | bytes 983048 | tf_op jit(solution)/shard_map/ppermute | solution.py:25
  45.9 6.4 %collective-permute-done.12.refs_1_ = bf16[2,2,64,640]{3,2,1,0:T(8,128)(2,1)S(1)} collective-permute-done((bf16[2,2,64,640]{3,2,1,0:T(8,128)(2,1)S(1)}, bf16[2,2,64,640]{3,2,1,0:T(8,128)(2,1)S(1)}, u32[]{:S(2)}, u32[]{:S(2)}) %collective-permute-start.12) | collective-permute-done | bytes 327712 | tf_op jit(solution)/shard_map/ppermute | solution.py:25
  52.3 0.9 collective-permute-done.13.refs_2_
  53.2 7.5 %collective-permute-done.14.refs_3_ = bf16[2,2,64,640]{3,2,1,0:T(8,128)(2,1)S(1)} collective-permute-done((bf16[2,2,64,640]{3,2,1,0:T(8,128)(2,1)S(1)}, bf16[2,2,64,640]{3,2,1,0:T(8,128)(2,1)S(1)}, u32[]{:S(2)}, u32[]{:S(2)}) %collective-permute-start.14) | collective-permute-done | bytes 327712 | tf_op jit(solution)/shard_map/ppermute | solution.py:25
  60.7 0.8 shard_map.73
  61.6 2.9 %collective-permute-start.25 = (bf16[2,64,640]{2,1,0:T(8,128)(2,1)S(1)}, bf16[2,64,640]{2,1,0:T(8,128)(2,1)S(1)}, u32[]{:S(2)}, u32[]{:S(2)}) collective-permute-start(bf16[2,64,640]{2,1,0:T(8,128)(2,1)S(1)} %get-tuple-element.69.p0.refs_4_), channel_id=1, source_target_pairs={{0,16},{32,48},{64,80},{96,112},{4,20},{36,52},{68,84},{100,116},{... | collective-permute-start | bytes 491528 | tf_op jit(solution)/shard_map/ppermute | solution.py:25
  64.6 1.4 collective-permute-start.26
  65.9 1.8 %shard_map.68 = (bf16[64,640]{1,0:T(8,128)(2,1)S(1)}, bf16[64,640]{1,0:T(8,128)(2,1)S(1)}, bf16[64,640]{1,0:T(8,128)(2,1)S(1)}, f32[64,640]{1,0:T(8,128)S(1)}) custom-call(s32[4]{0:T(128)S(1)} %shard_map.67.s, bf16[256,2560]{1,0:T(8,128)(2,1)S(1)} %collective-permute-done.v.refs_2_, bf16[2560,640]{1,0:T(8,128)(2,1)S(1)} %copy-done), custom_call_target="tpu_custom_call" | custom-call | flops 838860800 | bytes 4997120 | tf_op jit(solution)/shard_map/pallas_call | solution.py:40
  67.8 1.8 %shard_map.69 = (bf16[1,2,64,640]{3,2,1,0:T(8,128)(2,1)S(1)}, bf16[1,2,64,640]{3,2,1,0:T(8,128)(2,1)S(1)}, bf16[1,2,64,640]{3,2,1,0:T(8,128)(2,1)S(1)}, f32[1,2,64,640]{3,2,1,0:T(8,128)S(1)}) custom-call(s32[4]{0:T(128)S(1)} %shard_map.67.s, bf16[256,2560]{1,0:T(8,128)(2,1)S(1)} %collective-permute-done.1.v.refs_3_, bf16[2560,640]{1,0:T(8,128)(2,1)S(1)} %copy-done, ...), custom_call_target="tpu_custom_call" | custom-call | flops 838860800 | bytes 5816320 | tf_op jit(solution)/shard_map/pallas_call | solution.py:40
  69.6 0.7 collective-permute-start.4
  70.3 2.4 %collective-permute-start.5 = (bf16[1,2,64,640]{3,2,1,0:T(8,128)(2,1)S(1)}, bf16[1,2,64,640]{3,2,1,0:T(8,128)(2,1)S(1)}, u32[]{:S(2)}, u32[]{:S(2)}) collective-permute-start(bf16[1,2,64,640]{3,2,1,0:T(8,128)(2,1)S(1)} %get-tuple-element.52), channel_id=1, source_target_pairs={{0,24},{32,56},{64,88},{96,120},{4,28},{36,60},{68,92},{100,124},{... | collective-permute-start | bytes 491528 | tf_op jit(solution)/shard_map/ppermute | solution.py:25
  72.7 1.8 %shard_map.79 = bf16[256,2560]{1,0:T(8,128)(2,1)S(1)} custom-call(s32[4]{0:T(128)S(1)} %shard_map.67.s, bf16[2,64,640]{2,1,0:T(8,128)(2,1)S(1)} %get-tuple-element.69.p0.refs_4_, bf16[2,64,640]{2,1,0:T(8,128)(2,1)S(1)} %collective-permute-done.24.p1.refs_5_, bf16[2,64,640]{2,1,0:T(8,128)(2,1)S(1)} %collective-permute-done.25.p2.refs_6_, ...), custom_call_target="tpu_custom_call" | custom-call | flops 838860800 | bytes 5242880 | tf_op jit(solution)/shard_map/pallas_call | solution.py:40
  74.5 0.1 collective-permute-start.27
  74.6 1.8 %shard_map.70 = (bf16[64,640]{1,0:T(8,128)(2,1)S(1)}, bf16[64,640]{1,0:T(8,128)(2,1)S(1)}, bf16[64,640]{1,0:T(8,128)(2,1)S(1)}, f32[64,640]{1,0:T(8,128)S(1)}) custom-call(s32[4]{0:T(128)S(1)} %shard_map.67.s, bf16[256,2560]{1,0:T(8,128)(2,1)S(1)} %collective-permute-done.2.v.refs_2_, bf16[640,2560]{1,0:T(8,128)(2,1)S(1)} %copy-done.1), custom_call_target="tpu_custom_call" | custom-call | flops 838860800 | bytes 4997120 | tf_op jit(solution)/shard_map/pallas_call | solution.py:40
  76.4 2.7 %collective-permute-start.6 = (bf16[1,2,64,640]{3,2,1,0:T(8,128)(2,1)S(1)}, bf16[1,2,64,640]{3,2,1,0:T(8,128)(2,1)S(1)}, u32[]{:S(2)}, u32[]{:S(2)}) collective-permute-start(bf16[1,2,64,640]{3,2,1,0:T(8,128)(2,1)S(1)} %get-tuple-element.53), channel_id=1, source_target_pairs={{0,16},{32,48},{64,80},{96,112},{4,20},{36,52},{68,84},{100,116},{... | collective-permute-start | bytes 491528 | tf_op jit(solution)/shard_map/ppermute | solution.py:25
  79.1 1.8 %shard_map.71 = (bf16[1,2,64,640]{3,2,1,0:T(8,128)(2,1)S(1)}, bf16[1,2,64,640]{3,2,1,0:T(8,128)(2,1)S(1)}, bf16[1,2,64,640]{3,2,1,0:T(8,128)(2,1)S(1)}, f32[1,2,64,640]{3,2,1,0:T(8,128)S(1)}) custom-call(s32[4]{0:T(128)S(1)} %shard_map.67.s, bf16[256,2560]{1,0:T(8,128)(2,1)S(1)} %collective-permute-done.3.v.refs_3_, bf16[640,2560]{1,0:T(8,128)(2,1)S(1)} %copy-done.1, ...), custom_call_target="tpu_custom_call" | custom-call | flops 838860800 | bytes 5816320 | tf_op jit(solution)/shard_map/pallas_call | solution.py:40
  80.9 1.3 collective-permute-start.7
  82.2 0.8 collective-permute-start.8
  83.0 1.1 collective-permute-start.9
  84.1 0.8 collective-permute-done.6.refs_4_
  84.9 3.2 %collective-permute-done.7.refs_5_ = bf16[1,2,64,640]{3,2,1,0:T(8,128)(2,1)S(1)} collective-permute-done((bf16[1,2,64,640]{3,2,1,0:T(8,128)(2,1)S(1)}, bf16[1,2,64,640]{3,2,1,0:T(8,128)(2,1)S(1)}, u32[]{:S(2)}, u32[]{:S(2)}) %collective-permute-start.7) | collective-permute-done | bytes 163872 | tf_op jit(solution)/shard_map/ppermute | solution.py:25
  88.1 1.2 collective-permute-done.8.refs_6_
  89.3 2.6 %collective-permute-done.9.refs_7_ = bf16[1,2,64,640]{3,2,1,0:T(8,128)(2,1)S(1)} collective-permute-done((bf16[1,2,64,640]{3,2,1,0:T(8,128)(2,1)S(1)}, bf16[1,2,64,640]{3,2,1,0:T(8,128)(2,1)S(1)}, u32[]{:S(2)}, u32[]{:S(2)}) %collective-permute-start.9) | collective-permute-done | bytes 163872 | tf_op jit(solution)/shard_map/ppermute | solution.py:25
  91.9 0.9 shard_map.74
  92.7 0.7 collective-permute-start.15
  93.4 3.6 %collective-permute-start.16 = (bf16[2,64,640]{2,1,0:T(8,128)(2,1)S(1)}, bf16[2,64,640]{2,1,0:T(8,128)(2,1)S(1)}, u32[]{:S(2)}, u32[]{:S(2)}) collective-permute-start(bf16[2,64,640]{2,1,0:T(8,128)(2,1)S(1)} %get-tuple-element.62.p0.refs_8_), channel_id=1, source_target_pairs={{0,16},{32,48},{64,80},{96,112},{4,20},{36,52},{68,84},{100,116},{... | collective-permute-start | bytes 491528 | tf_op jit(solution)/shard_map/ppermute | solution.py:25
  97.0 0.8 collective-permute-start.17
  97.8 2.2 %collective-permute-done.15.p1.refs_9_ = bf16[2,64,640]{2,1,0:T(8,128)(2,1)S(1)} collective-permute-done((bf16[2,64,640]{2,1,0:T(8,128)(2,1)S(1)}, bf16[2,64,640]{2,1,0:T(8,128)(2,1)S(1)}, u32[]{:S(2)}, u32[]{:S(2)}) %collective-permute-start.15) | collective-permute-done | bytes 163872 | tf_op jit(solution)/shard_map/ppermute | solution.py:25
  100.0 2.1 %collective-permute-done.16.p2.refs_10_ = bf16[2,64,640]{2,1,0:T(8,128)(2,1)S(1)} collective-permute-done((bf16[2,64,640]{2,1,0:T(8,128)(2,1)S(1)}, bf16[2,64,640]{2,1,0:T(8,128)(2,1)S(1)}, u32[]{:S(2)}, u32[]{:S(2)}) %collective-permute-start.16) | collective-permute-done | bytes 163872 | tf_op jit(solution)/shard_map/ppermute | solution.py:25
  102.0 2.2 %collective-permute-done.17.p3.refs_11_ = bf16[2,64,640]{2,1,0:T(8,128)(2,1)S(1)} collective-permute-done((bf16[2,64,640]{2,1,0:T(8,128)(2,1)S(1)}, bf16[2,64,640]{2,1,0:T(8,128)(2,1)S(1)}, u32[]{:S(2)}, u32[]{:S(2)}) %collective-permute-start.17) | collective-permute-done | bytes 163872 | tf_op jit(solution)/shard_map/ppermute | solution.py:25
  104.2 1.8 %shard_map.76 = bf16[256,2560]{1,0:T(8,128)(2,1)S(1)} custom-call(s32[4]{0:T(128)S(1)} %shard_map.67.s, bf16[2,64,640]{2,1,0:T(8,128)(2,1)S(1)} %get-tuple-element.62.p0.refs_8_, bf16[2,64,640]{2,1,0:T(8,128)(2,1)S(1)} %collective-permute-done.15.p1.refs_9_, bf16[2,64,640]{2,1,0:T(8,128)(2,1)S(1)} %collective-permute-done.16.p2.refs_10_, ...), custom_call_target="tpu_custom_call" | custom-call | flops 838860800 | bytes 5242880 | tf_op jit(solution)/shard_map/pallas_call | solution.py:40
  106.0 0.1 collective-permute-start.18
  106.1 1.8 %shard_map.78.mine = f32[256,2560]{1,0:T(8,128)S(1)} custom-call(s32[4]{0:T(128)S(1)} %shard_map.67.s, bf16[2,64,640]{2,1,0:T(8,128)(2,1)S(1)} %get-tuple-element.69.p0.refs_4_, bf16[2,64,640]{2,1,0:T(8,128)(2,1)S(1)} %collective-permute-done.24.p1.refs_5_, bf16[2,64,640]{2,1,0:T(8,128)(2,1)S(1)} %collective-permute-done.25.p2.refs_6_, ...), custom_call_target="tpu_custom_call" | custom-call | flops 838860800 | bytes 6553600 | tf_op jit(solution)/shard_map/pallas_call | solution.py:40
  107.8 0.8 shard_map.80
  108.6 2.3 %collective-permute-start.28 = (bf16[128,2560]{1,0:T(8,128)(2,1)S(1)}, bf16[128,2560]{1,0:T(8,128)(2,1)S(1)}, u32[]{:S(2)}, u32[]{:S(2)}) collective-permute-start(bf16[128,2560]{1,0:T(8,128)(2,1)S(1)} %get-tuple-element.71), channel_id=1, source_target_pairs={{0,4},{32,36},{64,68},{96,100},{4,0},{36,32},{68,64},{100,96},{1,5... | collective-permute-start | bytes 1966088 | tf_op jit(solution)/shard_map/ppermute | solution.py:25
  110.9 1.7 %shard_map.75.mine = f32[256,2560]{1,0:T(8,128)S(1)} custom-call(s32[4]{0:T(128)S(1)} %shard_map.67.s, bf16[2,64,640]{2,1,0:T(8,128)(2,1)S(1)} %get-tuple-element.62.p0.refs_8_, bf16[2,64,640]{2,1,0:T(8,128)(2,1)S(1)} %collective-permute-done.15.p1.refs_9_, bf16[2,64,640]{2,1,0:T(8,128)(2,1)S(1)} %collective-permute-done.16.p2.refs_10_, ...), custom_call_target="tpu_custom_call" | custom-call | flops 838860800 | bytes 6553600 | tf_op jit(solution)/shard_map/pallas_call | solution.py:40
  112.7 0.8 shard_map.77
  113.4 0.3 collective-permute-start.19
  113.7 1.8 %collective-permute-start.20 = (bf16[2,32,1280]{2,1,0:T(8,128)(2,1)S(1)}, bf16[2,32,1280]{2,1,0:T(8,128)(2,1)S(1)}, u32[]{:S(2)}, u32[]{:S(2)}) collective-permute-start(bf16[2,32,1280]{2,1,0:T(8,128)(2,1)S(1)} %get-tuple-element.65), channel_id=1, source_target_pairs={{0,3},{32,35},{64,67},{96,99},{4,7},{36,39},{68,71},{100,103},{1,0... | collective-permute-start | bytes 491528 | tf_op jit(solution)/shard_map/ppermute | solution.py:25
  115.5 1.2 collective-permute-start.21
  116.8 2.2 %collective-permute-start.22 = (bf16[128,1280]{1,0:T(8,128)(2,1)S(1)}, bf16[128,1280]{1,0:T(8,128)(2,1)S(1)}, u32[]{:S(2)}, u32[]{:S(2)}) collective-permute-start(bf16[128,1280]{1,0:T(8,128)(2,1)S(1)} %get-tuple-element.67), channel_id=1, source_target_pairs={{0,64},{32,96},{64,4},{96,36},{4,68},{36,100},{68,0},{100,32},{1,6... | collective-permute-start | bytes 983048 | tf_op jit(solution)/shard_map/ppermute | solution.py:25
  119.0 8.8 %collective-permute-done.28.got = bf16[128,2560]{1,0:T(8,128)(2,1)S(1)} collective-permute-done((bf16[128,2560]{1,0:T(8,128)(2,1)S(1)}, bf16[128,2560]{1,0:T(8,128)(2,1)S(1)}, u32[]{:S(2)}, u32[]{:S(2)}) %collective-permute-start.28) | collective-permute-done | bytes 655392 | tf_op jit(solution)/shard_map/ppermute | solution.py:25
  127.8 3.1 %collective-permute-start.23 = (bf16[128,1280]{1,0:T(8,128)(2,1)S(1)}, bf16[128,1280]{1,0:T(8,128)(2,1)S(1)}, u32[]{:S(2)}, u32[]{:S(2)}) collective-permute-start(bf16[128,1280]{1,0:T(8,128)(2,1)S(1)} %get-tuple-element.68), channel_id=1, source_target_pairs={{0,68},{32,100},{64,0},{96,32},{4,64},{36,96},{68,4},{100,36},{1,6... | collective-permute-start | bytes 983048 | tf_op jit(solution)/shard_map/ppermute | solution.py:25
  130.9 0.6 collective-permute-start.34
  131.5 3.3 %collective-permute-start.35 = (bf16[2,2,64,640]{3,2,1,0:T(8,128)(2,1)S(1)}, bf16[2,2,64,640]{3,2,1,0:T(8,128)(2,1)S(1)}, u32[]{:S(2)}, u32[]{:S(2)}) collective-permute-start(bf16[2,2,64,640]{3,2,1,0:T(8,128)(2,1)S(1)} %get-tuple-element.78.refs_4_), channel_id=1, source_target_pairs={{0,16},{32,48},{64,80},{96,112},{4,20},{36,52},{68,84},{100,116},{... | collective-permute-start | bytes 983048 | tf_op jit(solution)/shard_map/ppermute | solution.py:25
  134.8 1.7 %collective-permute-start.36 = (bf16[2,2,64,640]{3,2,1,0:T(8,128)(2,1)S(1)}, bf16[2,2,64,640]{3,2,1,0:T(8,128)(2,1)S(1)}, u32[]{:S(2)}, u32[]{:S(2)}) collective-permute-start(bf16[2,2,64,640]{3,2,1,0:T(8,128)(2,1)S(1)} %get-tuple-element.78.refs_4_), channel_id=1, source_target_pairs={{0,24},{32,56},{64,88},{96,120},{4,28},{36,60},{68,92},{100,124},{... | collective-permute-start | bytes 983048 | tf_op jit(solution)/shard_map/ppermute | solution.py:25
  136.5 7.5 %shard_map.83 = f32[2560,640]{1,0:T(8,128)} custom-call(s32[4]{0:T(128)S(1)} %shard_map.67.s, bf16[256,2560]{1,0:T(8,128)(2,1)S(1)} %copy-done.2, bf16[256,2560]{1,0:T(8,128)(2,1)} %collective-permute-done.10.refs_1_, bf16[256,2560]{1,0:T(8,128)(2,1)S(1)} %collective-permute-done.v.refs_2_, bf16[256,2560]{1,0:T(8,128)(2,1)S(1)} %collective-permute-done.1.v.refs_3_, ...), custom_call_target="tpu_custom_call" | custom-call | flops 3355443200 | bytes 13107200 | tf_op jit(solution)/shard_map/pallas_call | solution.py:170
  144.0 0.8 shard_map.81
  144.8 0.5 collective-permute-start.29
  145.3 1.8 %collective-permute-start.30 = (bf16[32,2560]{1,0:T(8,128)(2,1)S(1)}, bf16[32,2560]{1,0:T(8,128)(2,1)S(1)}, u32[]{:S(2)}, u32[]{:S(2)}) collective-permute-start(bf16[32,2560]{1,0:T(8,128)(2,1)S(1)} %get-tuple-element.74), channel_id=1, source_target_pairs={{0,3},{32,35},{64,67},{96,99},{4,7},{36,39},{68,71},{100,103},{1,0... | collective-permute-start | bytes 491528 | tf_op jit(solution)/shard_map/ppermute | solution.py:25
  147.1 1.2 collective-permute-start.31
  148.4 0.4 collective-permute-done.36.refs_7_
  148.7 2.9 %collective-permute-start.33 = (bf16[32,1280]{1,0:T(8,128)(2,1)S(1)}, bf16[32,1280]{1,0:T(8,128)(2,1)S(1)}, u32[]{:S(2)}, u32[]{:S(2)}) collective-permute-start(bf16[32,1280]{1,0:T(8,128)(2,1)S(1)} %get-tuple-element.77), channel_id=1, source_target_pairs={{0,68},{32,100},{64,0},{96,32},{4,64},{36,96},{68,4},{100,36},{1,6... | collective-permute-start | bytes 245768 | tf_op jit(solution)/shard_map/ppermute | solution.py:25
  151.6 6.8 %shard_map.84 = f32[640,2560]{1,0:T(8,128)} custom-call(s32[4]{0:T(128)S(1)} %shard_map.67.s, bf16[256,2560]{1,0:T(8,128)(2,1)S(1)} %copy-done.3, bf16[256,2560]{1,0:T(8,128)(2,1)} %collective-permute-done.11.refs_4_.refs_1_, bf16[256,2560]{1,0:T(8,128)(2,1)S(1)} %collective-permute-done.2.v.refs_2_, bf16[256,2560]{1,0:T(8,128)(2,1)S(1)} %collective-permute-done.3.v.refs_3_, ...), custom_call_target="tpu_custom_call" | custom-call | flops 3355443200 | bytes 13107200 | tf_op jit(solution)/shard_map/pallas_call | solution.py:170
  158.5 1.3 shard_map.82
  (37 shorter events, 0.3 us)
Async XLA Ops:
  0.6 19.5 %collective-permute-start = (bf16[256,2560]{1,0:T(8,128)(2,1)}, bf16[256,2560]{1,0:T(8,128)(2,1)S(1)}, u32[]{:S(2)}, u32[]{:S(2)}) collective-permute-start(bf16[256,2560]{1,0:T(8,128)(2,1)} %refs_0_.4), channel_id=1, source_target_pairs={{0,68},{32,96},{64,0},{96,36},{4,64},{36,100},{68,4},{100,32},{1,6... | collective-permute-start | bytes 3932168 | tf_op jit(solution)/shard_map/ppermute | solution.py:25
  4.7 29.5 %collective-permute-start.2 = (bf16[256,2560]{1,0:T(8,128)(2,1)}, bf16[256,2560]{1,0:T(8,128)(2,1)S(1)}, u32[]{:S(2)}, u32[]{:S(2)}) collective-permute-start(bf16[256,2560]{1,0:T(8,128)(2,1)} %refs_0_.5), channel_id=1, source_target_pairs={{0,68},{32,96},{64,0},{96,36},{4,64},{36,100},{68,4},{100,32},{1,6... | collective-permute-start | bytes 3932168 | tf_op jit(solution)/shard_map/ppermute | solution.py:25
  5.1 30.2 %collective-permute-start.10 = (bf16[256,2560]{1,0:T(8,128)(2,1)}, bf16[256,2560]{1,0:T(8,128)(2,1)}, u32[]{:S(2)}, u32[]{:S(2)}) collective-permute-start(bf16[256,2560]{1,0:T(8,128)(2,1)} %refs_0_.4), channel_id=1, source_target_pairs={{0,32},{32,0},{64,96},{96,64},{4,36},{36,4},{68,100},{100,68},{1,3... | collective-permute-start | bytes 3932168 | tf_op jit(solution)/shard_map/ppermute | solution.py:25
  5.1 30.2 %collective-permute-start.11 = (bf16[256,2560]{1,0:T(8,128)(2,1)}, bf16[256,2560]{1,0:T(8,128)(2,1)}, u32[]{:S(2)}, u32[]{:S(2)}) collective-permute-start(bf16[256,2560]{1,0:T(8,128)(2,1)} %refs_0_.5), channel_id=1, source_target_pairs={{0,32},{32,0},{64,96},{96,64},{4,36},{36,4},{68,100},{100,68},{1,3... | collective-permute-start | bytes 3932168 | tf_op jit(solution)/shard_map/ppermute | solution.py:25
  5.7 29.7 %copy-start = (bf16[2560,640]{1,0:T(8,128)(2,1)S(1)}, bf16[2560,640]{1,0:T(8,128)(2,1)}, u32[]{:S(2)}) copy-start(bf16[2560,640]{1,0:T(8,128)(2,1)} %w_ref.7) | copy-start | bytes 9830404
  5.7 29.7 %copy-start.1 = (bf16[640,2560]{1,0:T(8,128)(2,1)S(1)}, bf16[640,2560]{1,0:T(8,128)(2,1)}, u32[]{:S(2)}) copy-start(bf16[640,2560]{1,0:T(8,128)(2,1)} %refs_5_.1) | copy-start | bytes 9830404
  5.7 29.7 %copy-start.2 = (bf16[256,2560]{1,0:T(8,128)(2,1)S(1)}, bf16[256,2560]{1,0:T(8,128)(2,1)}, u32[]{:S(2)}) copy-start(bf16[256,2560]{1,0:T(8,128)(2,1)} %refs_0_.4) | copy-start | bytes 3932164
  5.7 29.7 %copy-start.3 = (bf16[256,2560]{1,0:T(8,128)(2,1)S(1)}, bf16[256,2560]{1,0:T(8,128)(2,1)}, u32[]{:S(2)}) copy-start(bf16[256,2560]{1,0:T(8,128)(2,1)} %refs_0_.5) | copy-start | bytes 3932164
  20.2 47.6 %collective-permute-start.1 = (bf16[256,2560]{1,0:T(8,128)(2,1)S(1)}, bf16[256,2560]{1,0:T(8,128)(2,1)S(1)}, u32[]{:S(2)}, u32[]{:S(2)}) collective-permute-start(bf16[256,2560]{1,0:T(8,128)(2,1)S(1)} %collective-permute-done.v.refs_2_), channel_id=1, source_target_pairs={{0,32},{32,0},{64,96},{96,64},{4,36},{36,4},{68,100},{100,68},{1,3... | collective-permute-start | bytes 3932168 | tf_op jit(solution)/shard_map/ppermute | solution.py:25
  34.2 44.9 %collective-permute-start.3 = (bf16[256,2560]{1,0:T(8,128)(2,1)S(1)}, bf16[256,2560]{1,0:T(8,128)(2,1)S(1)}, u32[]{:S(2)}, u32[]{:S(2)}) collective-permute-start(bf16[256,2560]{1,0:T(8,128)(2,1)S(1)} %collective-permute-done.2.v.refs_2_), channel_id=1, source_target_pairs={{0,32},{32,0},{64,96},{96,64},{4,36},{36,4},{68,100},{100,68},{1,3... | collective-permute-start | bytes 3932168 | tf_op jit(solution)/shard_map/ppermute | solution.py:25
  41.7 10.7 %collective-permute-start.12 = (bf16[2,2,64,640]{3,2,1,0:T(8,128)(2,1)S(1)}, bf16[2,2,64,640]{3,2,1,0:T(8,128)(2,1)S(1)}, u32[]{:S(2)}, u32[]{:S(2)}) collective-permute-start(bf16[2,2,64,640]{3,2,1,0:T(8,128)(2,1)S(1)} %get-tuple-element.58), channel_id=1, source_target_pairs={{0,8},{32,40},{64,72},{96,104},{4,12},{36,44},{68,76},{100,108},{1... | collective-permute-start | bytes 983048 | tf_op jit(solution)/shard_map/ppermute | solution.py:25
  43.2 10.0 %collective-permute-start.13 = (bf16[2,2,64,640]{3,2,1,0:T(8,128)(2,1)S(1)}, bf16[2,2,64,640]{3,2,1,0:T(8,128)(2,1)S(1)}, u32[]{:S(2)}, u32[]{:S(2)}) collective-permute-start(bf16[2,2,64,640]{3,2,1,0:T(8,128)(2,1)S(1)} %get-tuple-element.59), channel_id=1, source_target_pairs={{0,24},{32,56},{64,88},{96,120},{4,28},{36,60},{68,92},{100,124},{... | collective-permute-start | bytes 983048 | tf_op jit(solution)/shard_map/ppermute | solution.py:25
  43.7 17.0 %collective-permute-start.14 = (bf16[2,2,64,640]{3,2,1,0:T(8,128)(2,1)S(1)}, bf16[2,2,64,640]{3,2,1,0:T(8,128)(2,1)S(1)}, u32[]{:S(2)}, u32[]{:S(2)}) collective-permute-start(bf16[2,2,64,640]{3,2,1,0:T(8,128)(2,1)S(1)} %get-tuple-element.60), channel_id=1, source_target_pairs={{0,16},{32,48},{64,80},{96,112},{4,20},{36,52},{68,84},{100,116},{... | collective-permute-start | bytes 983048 | tf_op jit(solution)/shard_map/ppermute | solution.py:25
  61.5 8.7 %collective-permute-start.24 = (bf16[2,64,640]{2,1,0:T(8,128)(2,1)S(1)}, bf16[2,64,640]{2,1,0:T(8,128)(2,1)S(1)}, u32[]{:S(2)}, u32[]{:S(2)}) collective-permute-start(bf16[2,64,640]{2,1,0:T(8,128)(2,1)S(1)} %get-tuple-element.69.p0.refs_4_), channel_id=1, source_target_pairs={{0,8},{32,40},{64,72},{96,104},{4,12},{36,44},{68,76},{100,108},{1... | collective-permute-start | bytes 491528 | tf_op jit(solution)/shard_map/ppermute | solution.py:25
  61.6 11.0 %collective-permute-start.25 = (bf16[2,64,640]{2,1,0:T(8,128)(2,1)S(1)}, bf16[2,64,640]{2,1,0:T(8,128)(2,1)S(1)}, u32[]{:S(2)}, u32[]{:S(2)}) collective-permute-start(bf16[2,64,640]{2,1,0:T(8,128)(2,1)S(1)} %get-tuple-element.69.p0.refs_4_), channel_id=1, source_target_pairs={{0,16},{32,48},{64,80},{96,112},{4,20},{36,52},{68,84},{100,116},{... | collective-permute-start | bytes 491528 | tf_op jit(solution)/shard_map/ppermute | solution.py:25
  64.6 8.1 %collective-permute-start.26 = (bf16[2,64,640]{2,1,0:T(8,128)(2,1)S(1)}, bf16[2,64,640]{2,1,0:T(8,128)(2,1)S(1)}, u32[]{:S(2)}, u32[]{:S(2)}) collective-permute-start(bf16[2,64,640]{2,1,0:T(8,128)(2,1)S(1)} %get-tuple-element.69.p0.refs_4_), channel_id=1, source_target_pairs={{0,24},{32,56},{64,88},{96,120},{4,28},{36,60},{68,92},{100,124},{... | collective-permute-start | bytes 491528 | tf_op jit(solution)/shard_map/ppermute | solution.py:25
  69.6 12.7 %collective-permute-start.4 = (bf16[1,2,64,640]{3,2,1,0:T(8,128)(2,1)S(1)}, bf16[1,2,64,640]{3,2,1,0:T(8,128)(2,1)S(1)}, u32[]{:S(2)}, u32[]{:S(2)}) collective-permute-start(bf16[1,2,64,640]{3,2,1,0:T(8,128)(2,1)S(1)} %get-tuple-element.51), channel_id=1, source_target_pairs={{0,8},{32,40},{64,72},{96,104},{4,12},{36,44},{68,76},{100,108},{1... | collective-permute-start | bytes 491528 | tf_op jit(solution)/shard_map/ppermute | solution.py:25
  70.3 12.8 %collective-permute-start.5 = (bf16[1,2,64,640]{3,2,1,0:T(8,128)(2,1)S(1)}, bf16[1,2,64,640]{3,2,1,0:T(8,128)(2,1)S(1)}, u32[]{:S(2)}, u32[]{:S(2)}) collective-permute-start(bf16[1,2,64,640]{3,2,1,0:T(8,128)(2,1)S(1)} %get-tuple-element.52), channel_id=1, source_target_pairs={{0,24},{32,56},{64,88},{96,120},{4,28},{36,60},{68,92},{100,124},{... | collective-permute-start | bytes 491528 | tf_op jit(solution)/shard_map/ppermute | solution.py:25
  74.5 33.3 %collective-permute-start.27 = (bf16[256,2560]{1,0:T(8,128)(2,1)S(1)}, bf16[256,2560]{1,0:T(8,128)(2,1)S(1)}, u32[]{:S(2)}, u32[]{:S(2)}) collective-permute-start(bf16[256,2560]{1,0:T(8,128)(2,1)S(1)} %shard_map.79), channel_id=1, source_target_pairs={{0,32},{32,0},{64,96},{96,64},{4,36},{36,4},{68,100},{100,68},{1,3... | collective-permute-start | bytes 3932168 | tf_op jit(solution)/shard_map/ppermute | solution.py:25
  76.4 8.5 %collective-permute-start.6 = (bf16[1,2,64,640]{3,2,1,0:T(8,128)(2,1)S(1)}, bf16[1,2,64,640]{3,2,1,0:T(8,128)(2,1)S(1)}, u32[]{:S(2)}, u32[]{:S(2)}) collective-permute-start(bf16[1,2,64,640]{3,2,1,0:T(8,128)(2,1)S(1)} %get-tuple-element.53), channel_id=1, source_target_pairs={{0,16},{32,48},{64,80},{96,112},{4,20},{36,52},{68,84},{100,116},{... | collective-permute-start | bytes 491528 | tf_op jit(solution)/shard_map/ppermute | solution.py:25
  80.9 7.1 %collective-permute-start.7 = (bf16[1,2,64,640]{3,2,1,0:T(8,128)(2,1)S(1)}, bf16[1,2,64,640]{3,2,1,0:T(8,128)(2,1)S(1)}, u32[]{:S(2)}, u32[]{:S(2)}) collective-permute-start(bf16[1,2,64,640]{3,2,1,0:T(8,128)(2,1)S(1)} %get-tuple-element.54), channel_id=1, source_target_pairs={{0,8},{32,40},{64,72},{96,104},{4,12},{36,44},{68,76},{100,108},{1... | collective-permute-start | bytes 491528 | tf_op jit(solution)/shard_map/ppermute | solution.py:25
  82.2 7.0 %collective-permute-start.8 = (bf16[1,2,64,640]{3,2,1,0:T(8,128)(2,1)S(1)}, bf16[1,2,64,640]{3,2,1,0:T(8,128)(2,1)S(1)}, u32[]{:S(2)}, u32[]{:S(2)}) collective-permute-start(bf16[1,2,64,640]{3,2,1,0:T(8,128)(2,1)S(1)} %get-tuple-element.55), channel_id=1, source_target_pairs={{0,24},{32,56},{64,88},{96,120},{4,28},{36,60},{68,92},{100,124},{... | collective-permute-start | bytes 491528 | tf_op jit(solution)/shard_map/ppermute | solution.py:25
  83.0 8.8 %collective-permute-start.9 = (bf16[1,2,64,640]{3,2,1,0:T(8,128)(2,1)S(1)}, bf16[1,2,64,640]{3,2,1,0:T(8,128)(2,1)S(1)}, u32[]{:S(2)}, u32[]{:S(2)}) collective-permute-start(bf16[1,2,64,640]{3,2,1,0:T(8,128)(2,1)S(1)} %get-tuple-element.56), channel_id=1, source_target_pairs={{0,16},{32,48},{64,80},{96,112},{4,20},{36,52},{68,84},{100,116},{... | collective-permute-start | bytes 491528 | tf_op jit(solution)/shard_map/ppermute | solution.py:25
  92.7 7.2 %collective-permute-start.15 = (bf16[2,64,640]{2,1,0:T(8,128)(2,1)S(1)}, bf16[2,64,640]{2,1,0:T(8,128)(2,1)S(1)}, u32[]{:S(2)}, u32[]{:S(2)}) collective-permute-start(bf16[2,64,640]{2,1,0:T(8,128)(2,1)S(1)} %get-tuple-element.62.p0.refs_8_), channel_id=1, source_target_pairs={{0,8},{32,40},{64,72},{96,104},{4,12},{36,44},{68,76},{100,108},{1... | collective-permute-start | bytes 491528 | tf_op jit(solution)/shard_map/ppermute | solution.py:25
  93.4 8.6 %collective-permute-start.16 = (bf16[2,64,640]{2,1,0:T(8,128)(2,1)S(1)}, bf16[2,64,640]{2,1,0:T(8,128)(2,1)S(1)}, u32[]{:S(2)}, u32[]{:S(2)}) collective-permute-start(bf16[2,64,640]{2,1,0:T(8,128)(2,1)S(1)} %get-tuple-element.62.p0.refs_8_), channel_id=1, source_target_pairs={{0,16},{32,48},{64,80},{96,112},{4,20},{36,52},{68,84},{100,116},{... | collective-permute-start | bytes 491528 | tf_op jit(solution)/shard_map/ppermute | solution.py:25
  97.0 7.2 %collective-permute-start.17 = (bf16[2,64,640]{2,1,0:T(8,128)(2,1)S(1)}, bf16[2,64,640]{2,1,0:T(8,128)(2,1)S(1)}, u32[]{:S(2)}, u32[]{:S(2)}) collective-permute-start(bf16[2,64,640]{2,1,0:T(8,128)(2,1)S(1)} %get-tuple-element.62.p0.refs_8_), channel_id=1, source_target_pairs={{0,24},{32,56},{64,88},{96,120},{4,28},{36,60},{68,92},{100,124},{... | collective-permute-start | bytes 491528 | tf_op jit(solution)/shard_map/ppermute | solution.py:25
  106.0 6.7 %collective-permute-start.18 = (bf16[256,2560]{1,0:T(8,128)(2,1)S(1)}, bf16[256,2560]{1,0:T(8,128)(2,1)S(1)}, u32[]{:S(2)}, u32[]{:S(2)}) collective-permute-start(bf16[256,2560]{1,0:T(8,128)(2,1)S(1)} %shard_map.76), channel_id=1, source_target_pairs={{0,32},{32,0},{64,96},{96,64},{4,36},{36,4},{68,100},{100,68},{1,3... | collective-permute-start | bytes 3932168 | tf_op jit(solution)/shard_map/ppermute | solution.py:25
  108.6 19.2 %collective-permute-start.28 = (bf16[128,2560]{1,0:T(8,128)(2,1)S(1)}, bf16[128,2560]{1,0:T(8,128)(2,1)S(1)}, u32[]{:S(2)}, u32[]{:S(2)}) collective-permute-start(bf16[128,2560]{1,0:T(8,128)(2,1)S(1)} %get-tuple-element.71), channel_id=1, source_target_pairs={{0,4},{32,36},{64,68},{96,100},{4,0},{36,32},{68,64},{100,96},{1,5... | collective-permute-start | bytes 1966088 | tf_op jit(solution)/shard_map/ppermute | solution.py:25
  113.4 17.5 %collective-permute-start.19 = (bf16[2,32,1280]{2,1,0:T(8,128)(2,1)S(1)}, bf16[2,32,1280]{2,1,0:T(8,128)(2,1)S(1)}, u32[]{:S(2)}, u32[]{:S(2)}) collective-permute-start(bf16[2,32,1280]{2,1,0:T(8,128)(2,1)S(1)} %get-tuple-element.64), channel_id=1, source_target_pairs={{0,1},{32,33},{64,65},{96,97},{4,5},{36,37},{68,69},{100,101},{1,2... | collective-permute-start | bytes 491528 | tf_op jit(solution)/shard_map/ppermute | solution.py:25
  113.7 17.8 %collective-permute-start.20 = (bf16[2,32,1280]{2,1,0:T(8,128)(2,1)S(1)}, bf16[2,32,1280]{2,1,0:T(8,128)(2,1)S(1)}, u32[]{:S(2)}, u32[]{:S(2)}) collective-permute-start(bf16[2,32,1280]{2,1,0:T(8,128)(2,1)S(1)} %get-tuple-element.65), channel_id=1, source_target_pairs={{0,3},{32,35},{64,67},{96,99},{4,7},{36,39},{68,71},{100,103},{1,0... | collective-permute-start | bytes 491528 | tf_op jit(solution)/shard_map/ppermute | solution.py:25
  115.5 19.2 %collective-permute-start.21 = (bf16[2,32,1280]{2,1,0:T(8,128)(2,1)S(1)}, bf16[2,32,1280]{2,1,0:T(8,128)(2,1)S(1)}, u32[]{:S(2)}, u32[]{:S(2)}) collective-permute-start(bf16[2,32,1280]{2,1,0:T(8,128)(2,1)S(1)} %get-tuple-element.66), channel_id=1, source_target_pairs={{0,2},{32,34},{64,66},{96,98},{4,6},{36,38},{68,70},{100,102},{1,3... | collective-permute-start | bytes 491528 | tf_op jit(solution)/shard_map/ppermute | solution.py:25
  116.8 27.2 %collective-permute-start.22 = (bf16[128,1280]{1,0:T(8,128)(2,1)S(1)}, bf16[128,1280]{1,0:T(8,128)(2,1)S(1)}, u32[]{:S(2)}, u32[]{:S(2)}) collective-permute-start(bf16[128,1280]{1,0:T(8,128)(2,1)S(1)} %get-tuple-element.67), channel_id=1, source_target_pairs={{0,64},{32,96},{64,4},{96,36},{4,68},{36,100},{68,0},{100,32},{1,6... | collective-permute-start | bytes 983048 | tf_op jit(solution)/shard_map/ppermute | solution.py:25
  127.8 16.2 %collective-permute-start.23 = (bf16[128,1280]{1,0:T(8,128)(2,1)S(1)}, bf16[128,1280]{1,0:T(8,128)(2,1)S(1)}, u32[]{:S(2)}, u32[]{:S(2)}) collective-permute-start(bf16[128,1280]{1,0:T(8,128)(2,1)S(1)} %get-tuple-element.68), channel_id=1, source_target_pairs={{0,68},{32,100},{64,0},{96,32},{4,64},{36,96},{68,4},{100,36},{1,6... | collective-permute-start | bytes 983048 | tf_op jit(solution)/shard_map/ppermute | solution.py:25
  130.9 16.2 %collective-permute-start.34 = (bf16[2,2,64,640]{3,2,1,0:T(8,128)(2,1)S(1)}, bf16[2,2,64,640]{3,2,1,0:T(8,128)(2,1)S(1)}, u32[]{:S(2)}, u32[]{:S(2)}) collective-permute-start(bf16[2,2,64,640]{3,2,1,0:T(8,128)(2,1)S(1)} %get-tuple-element.78.refs_4_), channel_id=1, source_target_pairs={{0,8},{32,40},{64,72},{96,104},{4,12},{36,44},{68,76},{100,108},{1... | collective-permute-start | bytes 983048 | tf_op jit(solution)/shard_map/ppermute | solution.py:25
  131.5 16.9 %collective-permute-start.35 = (bf16[2,2,64,640]{3,2,1,0:T(8,128)(2,1)S(1)}, bf16[2,2,64,640]{3,2,1,0:T(8,128)(2,1)S(1)}, u32[]{:S(2)}, u32[]{:S(2)}) collective-permute-start(bf16[2,2,64,640]{3,2,1,0:T(8,128)(2,1)S(1)} %get-tuple-element.78.refs_4_), channel_id=1, source_target_pairs={{0,16},{32,48},{64,80},{96,112},{4,20},{36,52},{68,84},{100,116},{... | collective-permute-start | bytes 983048 | tf_op jit(solution)/shard_map/ppermute | solution.py:25
  134.8 14.0 %collective-permute-start.36 = (bf16[2,2,64,640]{3,2,1,0:T(8,128)(2,1)S(1)}, bf16[2,2,64,640]{3,2,1,0:T(8,128)(2,1)S(1)}, u32[]{:S(2)}, u32[]{:S(2)}) collective-permute-start(bf16[2,2,64,640]{3,2,1,0:T(8,128)(2,1)S(1)} %get-tuple-element.78.refs_4_), channel_id=1, source_target_pairs={{0,24},{32,56},{64,88},{96,120},{4,28},{36,60},{68,92},{100,124},{... | collective-permute-start | bytes 983048 | tf_op jit(solution)/shard_map/ppermute | solution.py:25
  144.8 13.6 %collective-permute-start.29 = (bf16[32,2560]{1,0:T(8,128)(2,1)S(1)}, bf16[32,2560]{1,0:T(8,128)(2,1)S(1)}, u32[]{:S(2)}, u32[]{:S(2)}) collective-permute-start(bf16[32,2560]{1,0:T(8,128)(2,1)S(1)} %get-tuple-element.73), channel_id=1, source_target_pairs={{0,1},{32,33},{64,65},{96,97},{4,5},{36,37},{68,69},{100,101},{1,2... | collective-permute-start | bytes 491528 | tf_op jit(solution)/shard_map/ppermute | solution.py:25
  145.3 13.1 %collective-permute-start.30 = (bf16[32,2560]{1,0:T(8,128)(2,1)S(1)}, bf16[32,2560]{1,0:T(8,128)(2,1)S(1)}, u32[]{:S(2)}, u32[]{:S(2)}) collective-permute-start(bf16[32,2560]{1,0:T(8,128)(2,1)S(1)} %get-tuple-element.74), channel_id=1, source_target_pairs={{0,3},{32,35},{64,67},{96,99},{4,7},{36,39},{68,71},{100,103},{1,0... | collective-permute-start | bytes 491528 | tf_op jit(solution)/shard_map/ppermute | solution.py:25
  147.1 11.3 %collective-permute-start.31 = (bf16[32,2560]{1,0:T(8,128)(2,1)S(1)}, bf16[32,2560]{1,0:T(8,128)(2,1)S(1)}, u32[]{:S(2)}, u32[]{:S(2)}) collective-permute-start(bf16[32,2560]{1,0:T(8,128)(2,1)S(1)} %get-tuple-element.75), channel_id=1, source_target_pairs={{0,2},{32,34},{64,66},{96,98},{4,6},{36,38},{68,70},{100,102},{1,3... | collective-permute-start | bytes 491528 | tf_op jit(solution)/shard_map/ppermute | solution.py:25
  148.4 10.1 %collective-permute-start.32 = (bf16[32,1280]{1,0:T(8,128)(2,1)S(1)}, bf16[32,1280]{1,0:T(8,128)(2,1)S(1)}, u32[]{:S(2)}, u32[]{:S(2)}) collective-permute-start(bf16[32,1280]{1,0:T(8,128)(2,1)S(1)} %get-tuple-element.76), channel_id=1, source_target_pairs={{0,64},{32,96},{64,4},{96,36},{4,68},{36,100},{68,0},{100,32},{1,6... | collective-permute-start | bytes 245768 | tf_op jit(solution)/shard_map/ppermute | solution.py:25
  148.7 9.7 %collective-permute-start.33 = (bf16[32,1280]{1,0:T(8,128)(2,1)S(1)}, bf16[32,1280]{1,0:T(8,128)(2,1)S(1)}, u32[]{:S(2)}, u32[]{:S(2)}) collective-permute-start(bf16[32,1280]{1,0:T(8,128)(2,1)S(1)} %get-tuple-element.77), channel_id=1, source_target_pairs={{0,68},{32,100},{64,0},{96,32},{4,64},{36,96},{68,4},{100,36},{1,6... | collective-permute-start | bytes 245768 | tf_op jit(solution)/shard_map/ppermute | solution.py:25

commit v3 on v2

--- a/solution.py
+++ b/solution.py
@@ -57,8 +57,9 @@
     return refs[0][...] if len(refs) == 1 else jnp.concatenate([r[...] for r in refs], axis=0)
 
 
-def project(scal, jobs):
-    args, flops = [], 0
+def project(scal, jobs, prior=()):
+    args, flops = list(prior), 0
+    first = prior[0].shape[0] if prior else 0
     for blocks, w, _ in jobs:
         args += [*blocks, w]
         flops += 2 * sum(v.shape[0] for v in blocks) * w.size
@@ -69,8 +70,10 @@
     def body(s, *refs):
         x = s[0]
         outs, keep, part = refs[-5:-2], refs[-2], refs[-1]
-        at = 0
-        for a, (blocks, _, dim) in enumerate(jobs):
+        at = len(prior)
+        for o, p in zip((*outs, keep), refs[:at]):
+            o[:first] = p[...]
+        for a, (blocks, _, dim) in enumerate(jobs, first):
             lhs = cat(refs[at : at + len(blocks)])
             w = refs[at + len(blocks)]
             at += len(blocks) + 1
@@ -80,10 +83,10 @@
                     o[a, b] = part[pl.ds(b * 4 * quarter + lax.rem(x + j, 4) * quarter, quarter), :].astype(BF)
                 keep[a, b] = part[pl.ds(b * 4 * quarter + x * quarter, quarter), :]
 
-    shape = (len(jobs), 2, quarter, hidden)
+    shape = (first + len(jobs), 2, quarter, hidden)
     *sent, keep = run(
         body, [(shape, BF)] * 3 + [(shape, F32)], scal, args, [pltpu.VMEM((rows, hidden), F32)], flops, 12 << 20)
-    return sent, keep
+    return [*sent, keep]
 
 
 def warm(scal):
@@ -227,8 +230,8 @@
     for v in (tokens, out_grad):
         partner.append(shift(v, k=1))
         far.append(shift(v, z=(3, 1)))
-    sent_l, keep_l = project(
-        scal, [((tokens, partner[0]), weight_in, 0), ((out_grad, partner[1]), weight_out, 1)])
+    prior = project(scal, [((tokens, partner[0]), weight_in, 0)])
+    *sent_l, keep_l = project(scal, [((out_grad, partner[1]), weight_out, 1)], prior)
     got_l = around(sent_l, "x")
     far_t = [far[0], shift(far[0], k=1)]
     prior = project_block(scal, far_t[0], weight_in, 0)

time: 162 us -> 163 us (level)
    pallas_call x15 -> x16, Pallas kernels: 25.8 us -> 27.1 us  [run(): pl.pallas_call(body, in_specs=[pl.BlockSpec(memory_space=pltpu.SMEM)] + [...]
  transfers between devices with their start and end apart: 37 -> 37, of which waited for: 15 -> 15; matrix products, arithmetic and copies ran while one was open for 0% -> 0% of each run, Pallas kernels for 25% -> 26%
where the time goes in v3:
time: 163 us; the launch traced here: 161 us
  waiting for transfers between devices  66.7 us (41%)
  starting transfers between devices  50.8 us (31%)
  Pallas kernels  42.5 us (26%)
    ppermute x37, waiting for transfers between devices, shift(): return lax.ppermute(v, AXES, pairs)  66.7 us
    ppermute x37, starting transfers between devices, shift(): return lax.ppermute(v, AXES, pairs)  50.8 us
    pallas_call x16, Pallas kernels, run(): pl.pallas_call(body, in_specs=[pl.BlockSpec(memory_space=pltpu.SMEM)] + [...  27.1 us
    pallas_call x2, Pallas kernels, weight_grad(): pl.pallas_call(body, grid=(width // tile,), in_specs=[pl.BlockSpec(memory...  14.3 us
  transfers between devices with their start and end apart: 37, of which 15 were waited for; matrix products, arithmetic and copies ran while one was open for 0% of the time, Pallas kernels for 26%

profile of v3, /device:TPU:26, one launch (start us, length us, event | category | flops | bytes accessed | tf_op | source)
XLA Modules:
  0.0 161.1 jit_solution(11937171845461453197)
XLA Ops:
  0.6 4.1 %collective-permute-start = (bf16[256,2560]{1,0:T(8,128)(2,1)}, bf16[256,2560]{1,0:T(8,128)(2,1)S(1)}, u32[]{:S(2)}, u32[]{:S(2)}) collective-permute-start(bf16[256,2560]{1,0:T(8,128)(2,1)} %refs_0_.4), channel_id=1, source_target_pairs={{0,68},{32,96},{64,0},{96,36},{4,64},{36,100},{68,4},{100,32},{1,6... | collective-permute-start | bytes 3932168 | tf_op jit(solution)/shard_map/ppermute | solution.py:25
  4.7 0.4 collective-permute-start.2
  5.1 0.5 collective-permute-start.11
  5.7 14.4 %collective-permute-done.v.refs_2_ = bf16[256,2560]{1,0:T(8,128)(2,1)S(1)} collective-permute-done((bf16[256,2560]{1,0:T(8,128)(2,1)}, bf16[256,2560]{1,0:T(8,128)(2,1)S(1)}, u32[]{:S(2)}, u32[]{:S(2)}) %collective-permute-start) | collective-permute-done | bytes 1310752 | tf_op jit(solution)/shard_map/ppermute | solution.py:25
  20.2 14.0 %collective-permute-done.2.v.refs_2_ = bf16[256,2560]{1,0:T(8,128)(2,1)S(1)} collective-permute-done((bf16[256,2560]{1,0:T(8,128)(2,1)}, bf16[256,2560]{1,0:T(8,128)(2,1)S(1)}, u32[]{:S(2)}, u32[]{:S(2)}) %collective-permute-start.2) | collective-permute-done | bytes 1310752 | tf_op jit(solution)/shard_map/ppermute | solution.py:25
  34.2 1.1 shard_map.67.s
  35.4 3.8 %shard_map.72 = (bf16[1,2,64,640]{3,2,1,0:T(8,128)(2,1)S(1)}, bf16[1,2,64,640]{3,2,1,0:T(8,128)(2,1)S(1)}, bf16[1,2,64,640]{3,2,1,0:T(8,128)(2,1)S(1)}, f32[1,2,64,640]{3,2,1,0:T(8,128)S(1)}) custom-call(s32[4]{0:T(128)S(1)} %shard_map.67.s, bf16[256,2560]{1,0:T(8,128)(2,1)S(1)} %copy-done.3, bf16[256,2560]{1,0:T(8,128)(2,1)} %collective-permute-done.10.refs_1_, ...), custom_call_target="tpu_custom_call" | custom-call | flops 1677721600 | bytes 6717440 | tf_op jit(solution)/shard_map/pallas_call | solution.py:40
  39.3 3.7 %shard_map.73 = (bf16[2,2,64,640]{3,2,1,0:T(8,128)(2,1)S(1)}, bf16[2,2,64,640]{3,2,1,0:T(8,128)(2,1)S(1)}, bf16[2,2,64,640]{3,2,1,0:T(8,128)(2,1)S(1)}, f32[2,2,64,640]{3,2,1,0:T(8,128)S(1)}) custom-call(s32[4]{0:T(128)S(1)} %shard_map.67.s, bf16[1,2,64,640]{3,2,1,0:T(8,128)(2,1)S(1)} %get-tuple-element.61.refs_0_, ...), custom_call_target="tpu_custom_call" | custom-call | flops 1677721600 | bytes 8355840 | tf_op jit(solution)/shard_map/pallas_call | solution.py:40
  43.0 1.6 collective-permute-start.12
  44.5 0.5 collective-permute-start.13
  45.1 2.1 %collective-permute-start.14 = (bf16[2,2,64,640]{3,2,1,0:T(8,128)(2,1)S(1)}, bf16[2,2,64,640]{3,2,1,0:T(8,128)(2,1)S(1)}, u32[]{:S(2)}, u32[]{:S(2)}) collective-permute-start(bf16[2,2,64,640]{3,2,1,0:T(8,128)(2,1)S(1)} %get-tuple-element.68), channel_id=1, source_target_pairs={{0,16},{32,48},{64,80},{96,112},{4,20},{36,52},{68,84},{100,116},{... | collective-permute-start | bytes 983048 | tf_op jit(solution)/shard_map/ppermute | solution.py:25
  47.2 6.4 %collective-permute-done.12.refs_1_ = bf16[2,2,64,640]{3,2,1,0:T(8,128)(2,1)S(1)} collective-permute-done((bf16[2,2,64,640]{3,2,1,0:T(8,128)(2,1)S(1)}, bf16[2,2,64,640]{3,2,1,0:T(8,128)(2,1)S(1)}, u32[]{:S(2)}, u32[]{:S(2)}) %collective-permute-start.12) | collective-permute-done | bytes 327712 | tf_op jit(solution)/shard_map/ppermute | solution.py:25
  53.6 0.9 collective-permute-done.13.refs_2_
  54.5 7.5 %collective-permute-done.14.refs_3_ = bf16[2,2,64,640]{3,2,1,0:T(8,128)(2,1)S(1)} collective-permute-done((bf16[2,2,64,640]{3,2,1,0:T(8,128)(2,1)S(1)}, bf16[2,2,64,640]{3,2,1,0:T(8,128)(2,1)S(1)}, u32[]{:S(2)}, u32[]{:S(2)}) %collective-permute-start.14) | collective-permute-done | bytes 327712 | tf_op jit(solution)/shard_map/ppermute | solution.py:25
  62.0 0.8 shard_map.74
  62.9 2.9 %collective-permute-start.25 = (bf16[2,64,640]{2,1,0:T(8,128)(2,1)S(1)}, bf16[2,64,640]{2,1,0:T(8,128)(2,1)S(1)}, u32[]{:S(2)}, u32[]{:S(2)}) collective-permute-start(bf16[2,64,640]{2,1,0:T(8,128)(2,1)S(1)} %get-tuple-element.77.p0.refs_4_), channel_id=1, source_target_pairs={{0,16},{32,48},{64,80},{96,112},{4,20},{36,52},{68,84},{100,116},{... | collective-permute-start | bytes 491528 | tf_op jit(solution)/shard_map/ppermute | solution.py:25
  65.9 1.4 collective-permute-start.26
  67.3 1.8 %shard_map.68 = (bf16[64,640]{1,0:T(8,128)(2,1)S(1)}, bf16[64,640]{1,0:T(8,128)(2,1)S(1)}, bf16[64,640]{1,0:T(8,128)(2,1)S(1)}, f32[64,640]{1,0:T(8,128)S(1)}) custom-call(s32[4]{0:T(128)S(1)} %shard_map.67.s, bf16[256,2560]{1,0:T(8,128)(2,1)S(1)} %collective-permute-done.v.refs_2_, bf16[2560,640]{1,0:T(8,128)(2,1)S(1)} %copy-done), custom_call_target="tpu_custom_call" | custom-call | flops 838860800 | bytes 4997120 | tf_op jit(solution)/shard_map/pallas_call | solution.py:40
  69.1 1.8 %shard_map.69 = (bf16[1,2,64,640]{3,2,1,0:T(8,128)(2,1)S(1)}, bf16[1,2,64,640]{3,2,1,0:T(8,128)(2,1)S(1)}, bf16[1,2,64,640]{3,2,1,0:T(8,128)(2,1)S(1)}, f32[1,2,64,640]{3,2,1,0:T(8,128)S(1)}) custom-call(s32[4]{0:T(128)S(1)} %shard_map.67.s, bf16[256,2560]{1,0:T(8,128)(2,1)S(1)} %collective-permute-done.1.v.refs_3_, bf16[2560,640]{1,0:T(8,128)(2,1)S(1)} %copy-done, ...), custom_call_target="tpu_custom_call" | custom-call | flops 838860800 | bytes 5816320 | tf_op jit(solution)/shard_map/pallas_call | solution.py:40
  70.9 0.7 collective-permute-start.4
  71.6 2.3 %collective-permute-start.5 = (bf16[1,2,64,640]{3,2,1,0:T(8,128)(2,1)S(1)}, bf16[1,2,64,640]{3,2,1,0:T(8,128)(2,1)S(1)}, u32[]{:S(2)}, u32[]{:S(2)}) collective-permute-start(bf16[1,2,64,640]{3,2,1,0:T(8,128)(2,1)S(1)} %get-tuple-element.56), channel_id=1, source_target_pairs={{0,24},{32,56},{64,88},{96,120},{4,28},{36,60},{68,92},{100,124},{... | collective-permute-start | bytes 491528 | tf_op jit(solution)/shard_map/ppermute | solution.py:25
  73.9 0.2 collective-permute-done.26.p3.refs_7_
  74.0 1.8 %shard_map.80 = bf16[256,2560]{1,0:T(8,128)(2,1)S(1)} custom-call(s32[4]{0:T(128)S(1)} %shard_map.67.s, bf16[2,64,640]{2,1,0:T(8,128)(2,1)S(1)} %get-tuple-element.77.p0.refs_4_, bf16[2,64,640]{2,1,0:T(8,128)(2,1)S(1)} %collective-permute-done.24.p1.refs_5_, bf16[2,64,640]{2,1,0:T(8,128)(2,1)S(1)} %collective-permute-done.25.p2.refs_6_, ...), custom_call_target="tpu_custom_call" | custom-call | flops 838860800 | bytes 5242880 | tf_op jit(solution)/shard_map/pallas_call | solution.py:40
  75.9 1.8 %shard_map.70 = (bf16[64,640]{1,0:T(8,128)(2,1)S(1)}, bf16[64,640]{1,0:T(8,128)(2,1)S(1)}, bf16[64,640]{1,0:T(8,128)(2,1)S(1)}, f32[64,640]{1,0:T(8,128)S(1)}) custom-call(s32[4]{0:T(128)S(1)} %shard_map.67.s, bf16[256,2560]{1,0:T(8,128)(2,1)S(1)} %collective-permute-done.2.v.refs_2_, bf16[640,2560]{1,0:T(8,128)(2,1)S(1)} %copy-done.1), custom_call_target="tpu_custom_call" | custom-call | flops 838860800 | bytes 4997120 | tf_op jit(solution)/shard_map/pallas_call | solution.py:40
  77.7 2.7 %collective-permute-start.6 = (bf16[1,2,64,640]{3,2,1,0:T(8,128)(2,1)S(1)}, bf16[1,2,64,640]{3,2,1,0:T(8,128)(2,1)S(1)}, u32[]{:S(2)}, u32[]{:S(2)}) collective-permute-start(bf16[1,2,64,640]{3,2,1,0:T(8,128)(2,1)S(1)} %get-tuple-element.57), channel_id=1, source_target_pairs={{0,16},{32,48},{64,80},{96,112},{4,20},{36,52},{68,84},{100,116},{... | collective-permute-start | bytes 491528 | tf_op jit(solution)/shard_map/ppermute | solution.py:25
  80.4 1.8 %shard_map.71 = (bf16[1,2,64,640]{3,2,1,0:T(8,128)(2,1)S(1)}, bf16[1,2,64,640]{3,2,1,0:T(8,128)(2,1)S(1)}, bf16[1,2,64,640]{3,2,1,0:T(8,128)(2,1)S(1)}, f32[1,2,64,640]{3,2,1,0:T(8,128)S(1)}) custom-call(s32[4]{0:T(128)S(1)} %shard_map.67.s, bf16[256,2560]{1,0:T(8,128)(2,1)S(1)} %collective-permute-done.3.v.refs_3_, bf16[640,2560]{1,0:T(8,128)(2,1)S(1)} %copy-done.1, ...), custom_call_target="tpu_custom_call" | custom-call | flops 838860800 | bytes 5816320 | tf_op jit(solution)/shard_map/pallas_call | solution.py:40
  82.2 1.3 collective-permute-start.7
  83.5 0.8 collective-permute-start.8
  84.3 1.1 collective-permute-start.9
  85.5 0.8 collective-permute-done.6.refs_4_
  86.2 3.2 %collective-permute-done.7.refs_5_ = bf16[1,2,64,640]{3,2,1,0:T(8,128)(2,1)S(1)} collective-permute-done((bf16[1,2,64,640]{3,2,1,0:T(8,128)(2,1)S(1)}, bf16[1,2,64,640]{3,2,1,0:T(8,128)(2,1)S(1)}, u32[]{:S(2)}, u32[]{:S(2)}) %collective-permute-start.7) | collective-permute-done | bytes 163872 | tf_op jit(solution)/shard_map/ppermute | solution.py:25
  89.4 1.2 collective-permute-done.8.refs_6_
  90.6 2.6 %collective-permute-done.9.refs_7_ = bf16[1,2,64,640]{3,2,1,0:T(8,128)(2,1)S(1)} collective-permute-done((bf16[1,2,64,640]{3,2,1,0:T(8,128)(2,1)S(1)}, bf16[1,2,64,640]{3,2,1,0:T(8,128)(2,1)S(1)}, u32[]{:S(2)}, u32[]{:S(2)}) %collective-permute-start.9) | collective-permute-done | bytes 163872 | tf_op jit(solution)/shard_map/ppermute | solution.py:25
  93.2 0.9 shard_map.75
  94.0 0.7 collective-permute-start.15
  94.7 3.5 %collective-permute-start.16 = (bf16[2,64,640]{2,1,0:T(8,128)(2,1)S(1)}, bf16[2,64,640]{2,1,0:T(8,128)(2,1)S(1)}, u32[]{:S(2)}, u32[]{:S(2)}) collective-permute-start(bf16[2,64,640]{2,1,0:T(8,128)(2,1)S(1)} %get-tuple-element.70.p0.refs_8_), channel_id=1, source_target_pairs={{0,16},{32,48},{64,80},{96,112},{4,20},{36,52},{68,84},{100,116},{... | collective-permute-start | bytes 491528 | tf_op jit(solution)/shard_map/ppermute | solution.py:25
  98.3 0.9 collective-permute-start.17
  99.1 2.1 %collective-permute-done.15.p1.refs_9_ = bf16[2,64,640]{2,1,0:T(8,128)(2,1)S(1)} collective-permute-done((bf16[2,64,640]{2,1,0:T(8,128)(2,1)S(1)}, bf16[2,64,640]{2,1,0:T(8,128)(2,1)S(1)}, u32[]{:S(2)}, u32[]{:S(2)}) %collective-permute-start.15) | collective-permute-done | bytes 163872 | tf_op jit(solution)/shard_map/ppermute | solution.py:25
  101.2 2.1 %collective-permute-done.16.p2.refs_10_ = bf16[2,64,640]{2,1,0:T(8,128)(2,1)S(1)} collective-permute-done((bf16[2,64,640]{2,1,0:T(8,128)(2,1)S(1)}, bf16[2,64,640]{2,1,0:T(8,128)(2,1)S(1)}, u32[]{:S(2)}, u32[]{:S(2)}) %collective-permute-start.16) | collective-permute-done | bytes 163872 | tf_op jit(solution)/shard_map/ppermute | solution.py:25
  103.3 2.2 %collective-permute-done.17.p3.refs_11_ = bf16[2,64,640]{2,1,0:T(8,128)(2,1)S(1)} collective-permute-done((bf16[2,64,640]{2,1,0:T(8,128)(2,1)S(1)}, bf16[2,64,640]{2,1,0:T(8,128)(2,1)S(1)}, u32[]{:S(2)}, u32[]{:S(2)}) %collective-permute-start.17) | collective-permute-done | bytes 163872 | tf_op jit(solution)/shard_map/ppermute | solution.py:25
  105.5 1.8 %shard_map.77 = bf16[256,2560]{1,0:T(8,128)(2,1)S(1)} custom-call(s32[4]{0:T(128)S(1)} %shard_map.67.s, bf16[2,64,640]{2,1,0:T(8,128)(2,1)S(1)} %get-tuple-element.70.p0.refs_8_, bf16[2,64,640]{2,1,0:T(8,128)(2,1)S(1)} %collective-permute-done.15.p1.refs_9_, bf16[2,64,640]{2,1,0:T(8,128)(2,1)S(1)} %collective-permute-done.16.p2.refs_10_, ...), custom_call_target="tpu_custom_call" | custom-call | flops 838860800 | bytes 5242880 | tf_op jit(solution)/shard_map/pallas_call | solution.py:40
  107.3 1.8 %shard_map.79.mine = f32[256,2560]{1,0:T(8,128)S(1)} custom-call(s32[4]{0:T(128)S(1)} %shard_map.67.s, bf16[2,64,640]{2,1,0:T(8,128)(2,1)S(1)} %get-tuple-element.77.p0.refs_4_, bf16[2,64,640]{2,1,0:T(8,128)(2,1)S(1)} %collective-permute-done.24.p1.refs_5_, bf16[2,64,640]{2,1,0:T(8,128)(2,1)S(1)} %collective-permute-done.25.p2.refs_6_, ...), custom_call_target="tpu_custom_call" | custom-call | flops 838860800 | bytes 6553600 | tf_op jit(solution)/shard_map/pallas_call | solution.py:40
  109.1 0.8 shard_map.81
  109.9 2.3 %collective-permute-start.28 = (bf16[128,2560]{1,0:T(8,128)(2,1)S(1)}, bf16[128,2560]{1,0:T(8,128)(2,1)S(1)}, u32[]{:S(2)}, u32[]{:S(2)}) collective-permute-start(bf16[128,2560]{1,0:T(8,128)(2,1)S(1)} %get-tuple-element.79), channel_id=1, source_target_pairs={{0,4},{32,36},{64,68},{96,100},{4,0},{36,32},{68,64},{100,96},{1,5... | collective-permute-start | bytes 1966088 | tf_op jit(solution)/shard_map/ppermute | solution.py:25
  112.2 1.7 %shard_map.76.mine = f32[256,2560]{1,0:T(8,128)S(1)} custom-call(s32[4]{0:T(128)S(1)} %shard_map.67.s, bf16[2,64,640]{2,1,0:T(8,128)(2,1)S(1)} %get-tuple-element.70.p0.refs_8_, bf16[2,64,640]{2,1,0:T(8,128)(2,1)S(1)} %collective-permute-done.15.p1.refs_9_, bf16[2,64,640]{2,1,0:T(8,128)(2,1)S(1)} %collective-permute-done.16.p2.refs_10_, ...), custom_call_target="tpu_custom_call" | custom-call | flops 838860800 | bytes 6553600 | tf_op jit(solution)/shard_map/pallas_call | solution.py:40
  113.9 0.8 shard_map.78
  114.7 0.3 collective-permute-start.19
  115.0 1.8 %collective-permute-start.20 = (bf16[2,32,1280]{2,1,0:T(8,128)(2,1)S(1)}, bf16[2,32,1280]{2,1,0:T(8,128)(2,1)S(1)}, u32[]{:S(2)}, u32[]{:S(2)}) collective-permute-start(bf16[2,32,1280]{2,1,0:T(8,128)(2,1)S(1)} %get-tuple-element.73), channel_id=1, source_target_pairs={{0,3},{32,35},{64,67},{96,99},{4,7},{36,39},{68,71},{100,103},{1,0... | collective-permute-start | bytes 491528 | tf_op jit(solution)/shard_map/ppermute | solution.py:25
  116.8 1.2 collective-permute-start.21
  118.0 2.2 %collective-permute-start.22 = (bf16[128,1280]{1,0:T(8,128)(2,1)S(1)}, bf16[128,1280]{1,0:T(8,128)(2,1)S(1)}, u32[]{:S(2)}, u32[]{:S(2)}) collective-permute-start(bf16[128,1280]{1,0:T(8,128)(2,1)S(1)} %get-tuple-element.75), channel_id=1, source_target_pairs={{0,64},{32,96},{64,4},{96,36},{4,68},{36,100},{68,0},{100,32},{1,6... | collective-permute-start | bytes 983048 | tf_op jit(solution)/shard_map/ppermute | solution.py:25
  120.3 8.8 %collective-permute-done.28.got = bf16[128,2560]{1,0:T(8,128)(2,1)S(1)} collective-permute-done((bf16[128,2560]{1,0:T(8,128)(2,1)S(1)}, bf16[128,2560]{1,0:T(8,128)(2,1)S(1)}, u32[]{:S(2)}, u32[]{:S(2)}) %collective-permute-start.28) | collective-permute-done | bytes 655392 | tf_op jit(solution)/shard_map/ppermute | solution.py:25
  129.1 3.1 %collective-permute-start.23 = (bf16[128,1280]{1,0:T(8,128)(2,1)S(1)}, bf16[128,1280]{1,0:T(8,128)(2,1)S(1)}, u32[]{:S(2)}, u32[]{:S(2)}) collective-permute-start(bf16[128,1280]{1,0:T(8,128)(2,1)S(1)} %get-tuple-element.76), channel_id=1, source_target_pairs={{0,68},{32,100},{64,0},{96,32},{4,64},{36,96},{68,4},{100,36},{1,6... | collective-permute-start | bytes 983048 | tf_op jit(solution)/shard_map/ppermute | solution.py:25
  132.2 0.6 collective-permute-start.34
  132.8 3.3 %collective-permute-start.35 = (bf16[2,2,64,640]{3,2,1,0:T(8,128)(2,1)S(1)}, bf16[2,2,64,640]{3,2,1,0:T(8,128)(2,1)S(1)}, u32[]{:S(2)}, u32[]{:S(2)}) collective-permute-start(bf16[2,2,64,640]{3,2,1,0:T(8,128)(2,1)S(1)} %get-tuple-element.86.refs_4_), channel_id=1, source_target_pairs={{0,16},{32,48},{64,80},{96,112},{4,20},{36,52},{68,84},{100,116},{... | collective-permute-start | bytes 983048 | tf_op jit(solution)/shard_map/ppermute | solution.py:25
  136.0 1.7 %collective-permute-start.36 = (bf16[2,2,64,640]{3,2,1,0:T(8,128)(2,1)S(1)}, bf16[2,2,64,640]{3,2,1,0:T(8,128)(2,1)S(1)}, u32[]{:S(2)}, u32[]{:S(2)}) collective-permute-start(bf16[2,2,64,640]{3,2,1,0:T(8,128)(2,1)S(1)} %get-tuple-element.86.refs_4_), channel_id=1, source_target_pairs={{0,24},{32,56},{64,88},{96,120},{4,28},{36,60},{68,92},{100,124},{... | collective-permute-start | bytes 983048 | tf_op jit(solution)/shard_map/ppermute | solution.py:25
  137.8 7.5 %shard_map.84 = f32[2560,640]{1,0:T(8,128)} custom-call(s32[4]{0:T(128)S(1)} %shard_map.67.s, bf16[256,2560]{1,0:T(8,128)(2,1)S(1)} %copy-done.3, bf16[256,2560]{1,0:T(8,128)(2,1)} %collective-permute-done.10.refs_1_, bf16[256,2560]{1,0:T(8,128)(2,1)S(1)} %collective-permute-done.v.refs_2_, bf16[256,2560]{1,0:T(8,128)(2,1)S(1)} %collective-permute-done.1.v.refs_3_, ...), custom_call_target="tpu_custom_call" | custom-call | flops 3355443200 | bytes 13107200 | tf_op jit(solution)/shard_map/pallas_call | solution.py:173
  145.3 0.8 shard_map.82
  146.1 0.5 collective-permute-start.29
  146.6 1.8 %collective-permute-start.30 = (bf16[32,2560]{1,0:T(8,128)(2,1)S(1)}, bf16[32,2560]{1,0:T(8,128)(2,1)S(1)}, u32[]{:S(2)}, u32[]{:S(2)}) collective-permute-start(bf16[32,2560]{1,0:T(8,128)(2,1)S(1)} %get-tuple-element.82), channel_id=1, source_target_pairs={{0,3},{32,35},{64,67},{96,99},{4,7},{36,39},{68,71},{100,103},{1,0... | collective-permute-start | bytes 491528 | tf_op jit(solution)/shard_map/ppermute | solution.py:25
  148.4 1.3 collective-permute-start.31
  149.7 0.3 collective-permute-done.36.refs_7_
  150.0 2.9 %collective-permute-start.33 = (bf16[32,1280]{1,0:T(8,128)(2,1)S(1)}, bf16[32,1280]{1,0:T(8,128)(2,1)S(1)}, u32[]{:S(2)}, u32[]{:S(2)}) collective-permute-start(bf16[32,1280]{1,0:T(8,128)(2,1)S(1)} %get-tuple-element.85), channel_id=1, source_target_pairs={{0,68},{32,100},{64,0},{96,32},{4,64},{36,96},{68,4},{100,36},{1,6... | collective-permute-start | bytes 245768 | tf_op jit(solution)/shard_map/ppermute | solution.py:25
  152.9 6.8 %shard_map.85 = f32[640,2560]{1,0:T(8,128)} custom-call(s32[4]{0:T(128)S(1)} %shard_map.67.s, bf16[256,2560]{1,0:T(8,128)(2,1)S(1)} %copy-done.2, bf16[256,2560]{1,0:T(8,128)(2,1)} %collective-permute-done.11.refs_5_.refs_1_, bf16[256,2560]{1,0:T(8,128)(2,1)S(1)} %collective-permute-done.2.v.refs_2_, bf16[256,2560]{1,0:T(8,128)(2,1)S(1)} %collective-permute-done.3.v.refs_3_, ...), custom_call_target="tpu_custom_call" | custom-call | flops 3355443200 | bytes 13107200 | tf_op jit(solution)/shard_map/pallas_call | solution.py:173
  159.8 1.3 shard_map.83
  (38 shorter events, 0.4 us)
Async XLA Ops:
  0.6 19.5 %collective-permute-start = (bf16[256,2560]{1,0:T(8,128)(2,1)}, bf16[256,2560]{1,0:T(8,128)(2,1)S(1)}, u32[]{:S(2)}, u32[]{:S(2)}) collective-permute-start(bf16[256,2560]{1,0:T(8,128)(2,1)} %refs_0_.4), channel_id=1, source_target_pairs={{0,68},{32,96},{64,0},{96,36},{4,64},{36,100},{68,4},{100,32},{1,6... | collective-permute-start | bytes 3932168 | tf_op jit(solution)/shard_map/ppermute | solution.py:25
  4.7 29.5 %collective-permute-start.2 = (bf16[256,2560]{1,0:T(8,128)(2,1)}, bf16[256,2560]{1,0:T(8,128)(2,1)S(1)}, u32[]{:S(2)}, u32[]{:S(2)}) collective-permute-start(bf16[256,2560]{1,0:T(8,128)(2,1)} %refs_0_.5), channel_id=1, source_target_pairs={{0,68},{32,96},{64,0},{96,36},{4,64},{36,100},{68,4},{100,32},{1,6... | collective-permute-start | bytes 3932168 | tf_op jit(solution)/shard_map/ppermute | solution.py:25
  5.1 30.3 %collective-permute-start.10 = (bf16[256,2560]{1,0:T(8,128)(2,1)}, bf16[256,2560]{1,0:T(8,128)(2,1)}, u32[]{:S(2)}, u32[]{:S(2)}) collective-permute-start(bf16[256,2560]{1,0:T(8,128)(2,1)} %refs_0_.4), channel_id=1, source_target_pairs={{0,32},{32,0},{64,96},{96,64},{4,36},{36,4},{68,100},{100,68},{1,3... | collective-permute-start | bytes 3932168 | tf_op jit(solution)/shard_map/ppermute | solution.py:25
  5.1 34.1 %collective-permute-start.11 = (bf16[256,2560]{1,0:T(8,128)(2,1)}, bf16[256,2560]{1,0:T(8,128)(2,1)}, u32[]{:S(2)}, u32[]{:S(2)}) collective-permute-start(bf16[256,2560]{1,0:T(8,128)(2,1)} %refs_0_.5), channel_id=1, source_target_pairs={{0,32},{32,0},{64,96},{96,64},{4,36},{36,4},{68,100},{100,68},{1,3... | collective-permute-start | bytes 3932168 | tf_op jit(solution)/shard_map/ppermute | solution.py:25
  5.7 29.7 %copy-start = (bf16[2560,640]{1,0:T(8,128)(2,1)S(1)}, bf16[2560,640]{1,0:T(8,128)(2,1)}, u32[]{:S(2)}) copy-start(bf16[2560,640]{1,0:T(8,128)(2,1)} %w_ref.7) | copy-start | bytes 9830404
  5.7 29.7 %copy-start.3 = (bf16[256,2560]{1,0:T(8,128)(2,1)S(1)}, bf16[256,2560]{1,0:T(8,128)(2,1)}, u32[]{:S(2)}) copy-start(bf16[256,2560]{1,0:T(8,128)(2,1)} %refs_0_.4) | copy-start | bytes 3932164
  20.2 48.9 %collective-permute-start.1 = (bf16[256,2560]{1,0:T(8,128)(2,1)S(1)}, bf16[256,2560]{1,0:T(8,128)(2,1)S(1)}, u32[]{:S(2)}, u32[]{:S(2)}) collective-permute-start(bf16[256,2560]{1,0:T(8,128)(2,1)S(1)} %collective-permute-done.v.refs_2_), channel_id=1, source_target_pairs={{0,32},{32,0},{64,96},{96,64},{4,36},{36,4},{68,100},{100,68},{1,3... | collective-permute-start | bytes 3932168 | tf_op jit(solution)/shard_map/ppermute | solution.py:25
  34.2 46.2 %collective-permute-start.3 = (bf16[256,2560]{1,0:T(8,128)(2,1)S(1)}, bf16[256,2560]{1,0:T(8,128)(2,1)S(1)}, u32[]{:S(2)}, u32[]{:S(2)}) collective-permute-start(bf16[256,2560]{1,0:T(8,128)(2,1)S(1)} %collective-permute-done.2.v.refs_2_), channel_id=1, source_target_pairs={{0,32},{32,0},{64,96},{96,64},{4,36},{36,4},{68,100},{100,68},{1,3... | collective-permute-start | bytes 3932168 | tf_op jit(solution)/shard_map/ppermute | solution.py:25
  35.4 3.9 %copy-start.1 = (bf16[640,2560]{1,0:T(8,128)(2,1)S(1)}, bf16[640,2560]{1,0:T(8,128)(2,1)}, u32[]{:S(2)}) copy-start(bf16[640,2560]{1,0:T(8,128)(2,1)} %refs_6_.1) | copy-start | bytes 9830404
  35.4 3.9 %copy-start.2 = (bf16[256,2560]{1,0:T(8,128)(2,1)S(1)}, bf16[256,2560]{1,0:T(8,128)(2,1)}, u32[]{:S(2)}) copy-start(bf16[256,2560]{1,0:T(8,128)(2,1)} %refs_0_.5) | copy-start | bytes 3932164
  43.0 10.7 %collective-permute-start.12 = (bf16[2,2,64,640]{3,2,1,0:T(8,128)(2,1)S(1)}, bf16[2,2,64,640]{3,2,1,0:T(8,128)(2,1)S(1)}, u32[]{:S(2)}, u32[]{:S(2)}) collective-permute-start(bf16[2,2,64,640]{3,2,1,0:T(8,128)(2,1)S(1)} %get-tuple-element.66), channel_id=1, source_target_pairs={{0,8},{32,40},{64,72},{96,104},{4,12},{36,44},{68,76},{100,108},{1... | collective-permute-start | bytes 983048 | tf_op jit(solution)/shard_map/ppermute | solution.py:25
  44.5 10.0 %collective-permute-start.13 = (bf16[2,2,64,640]{3,2,1,0:T(8,128)(2,1)S(1)}, bf16[2,2,64,640]{3,2,1,0:T(8,128)(2,1)S(1)}, u32[]{:S(2)}, u32[]{:S(2)}) collective-permute-start(bf16[2,2,64,640]{3,2,1,0:T(8,128)(2,1)S(1)} %get-tuple-element.67), channel_id=1, source_target_pairs={{0,24},{32,56},{64,88},{96,120},{4,28},{36,60},{68,92},{100,124},{... | collective-permute-start | bytes 983048 | tf_op jit(solution)/shard_map/ppermute | solution.py:25
  45.1 16.9 %collective-permute-start.14 = (bf16[2,2,64,640]{3,2,1,0:T(8,128)(2,1)S(1)}, bf16[2,2,64,640]{3,2,1,0:T(8,128)(2,1)S(1)}, u32[]{:S(2)}, u32[]{:S(2)}) collective-permute-start(bf16[2,2,64,640]{3,2,1,0:T(8,128)(2,1)S(1)} %get-tuple-element.68), channel_id=1, source_target_pairs={{0,16},{32,48},{64,80},{96,112},{4,20},{36,52},{68,84},{100,116},{... | collective-permute-start | bytes 983048 | tf_op jit(solution)/shard_map/ppermute | solution.py:25
  62.9 8.7 %collective-permute-start.24 = (bf16[2,64,640]{2,1,0:T(8,128)(2,1)S(1)}, bf16[2,64,640]{2,1,0:T(8,128)(2,1)S(1)}, u32[]{:S(2)}, u32[]{:S(2)}) collective-permute-start(bf16[2,64,640]{2,1,0:T(8,128)(2,1)S(1)} %get-tuple-element.77.p0.refs_4_), channel_id=1, source_target_pairs={{0,8},{32,40},{64,72},{96,104},{4,12},{36,44},{68,76},{100,108},{1... | collective-permute-start | bytes 491528 | tf_op jit(solution)/shard_map/ppermute | solution.py:25
  62.9 10.9 %collective-permute-start.25 = (bf16[2,64,640]{2,1,0:T(8,128)(2,1)S(1)}, bf16[2,64,640]{2,1,0:T(8,128)(2,1)S(1)}, u32[]{:S(2)}, u32[]{:S(2)}) collective-permute-start(bf16[2,64,640]{2,1,0:T(8,128)(2,1)S(1)} %get-tuple-element.77.p0.refs_4_), channel_id=1, source_target_pairs={{0,16},{32,48},{64,80},{96,112},{4,20},{36,52},{68,84},{100,116},{... | collective-permute-start | bytes 491528 | tf_op jit(solution)/shard_map/ppermute | solution.py:25
  65.9 8.1 %collective-permute-start.26 = (bf16[2,64,640]{2,1,0:T(8,128)(2,1)S(1)}, bf16[2,64,640]{2,1,0:T(8,128)(2,1)S(1)}, u32[]{:S(2)}, u32[]{:S(2)}) collective-permute-start(bf16[2,64,640]{2,1,0:T(8,128)(2,1)S(1)} %get-tuple-element.77.p0.refs_4_), channel_id=1, source_target_pairs={{0,24},{32,56},{64,88},{96,120},{4,28},{36,60},{68,92},{100,124},{... | collective-permute-start | bytes 491528 | tf_op jit(solution)/shard_map/ppermute | solution.py:25
  70.9 12.6 %collective-permute-start.4 = (bf16[1,2,64,640]{3,2,1,0:T(8,128)(2,1)S(1)}, bf16[1,2,64,640]{3,2,1,0:T(8,128)(2,1)S(1)}, u32[]{:S(2)}, u32[]{:S(2)}) collective-permute-start(bf16[1,2,64,640]{3,2,1,0:T(8,128)(2,1)S(1)} %get-tuple-element.55), channel_id=1, source_target_pairs={{0,8},{32,40},{64,72},{96,104},{4,12},{36,44},{68,76},{100,108},{1... | collective-permute-start | bytes 491528 | tf_op jit(solution)/shard_map/ppermute | solution.py:25
  71.6 12.7 %collective-permute-start.5 = (bf16[1,2,64,640]{3,2,1,0:T(8,128)(2,1)S(1)}, bf16[1,2,64,640]{3,2,1,0:T(8,128)(2,1)S(1)}, u32[]{:S(2)}, u32[]{:S(2)}) collective-permute-start(bf16[1,2,64,640]{3,2,1,0:T(8,128)(2,1)S(1)} %get-tuple-element.56), channel_id=1, source_target_pairs={{0,24},{32,56},{64,88},{96,120},{4,28},{36,60},{68,92},{100,124},{... | collective-permute-start | bytes 491528 | tf_op jit(solution)/shard_map/ppermute | solution.py:25
  75.8 33.3 %collective-permute-start.27 = (bf16[256,2560]{1,0:T(8,128)(2,1)S(1)}, bf16[256,2560]{1,0:T(8,128)(2,1)S(1)}, u32[]{:S(2)}, u32[]{:S(2)}) collective-permute-start(bf16[256,2560]{1,0:T(8,128)(2,1)S(1)} %shard_map.80), channel_id=1, source_target_pairs={{0,32},{32,0},{64,96},{96,64},{4,36},{36,4},{68,100},{100,68},{1,3... | collective-permute-start | bytes 3932168 | tf_op jit(solution)/shard_map/ppermute | solution.py:25
  77.7 8.5 %collective-permute-start.6 = (bf16[1,2,64,640]{3,2,1,0:T(8,128)(2,1)S(1)}, bf16[1,2,64,640]{3,2,1,0:T(8,128)(2,1)S(1)}, u32[]{:S(2)}, u32[]{:S(2)}) collective-permute-start(bf16[1,2,64,640]{3,2,1,0:T(8,128)(2,1)S(1)} %get-tuple-element.57), channel_id=1, source_target_pairs={{0,16},{32,48},{64,80},{96,112},{4,20},{36,52},{68,84},{100,116},{... | collective-permute-start | bytes 491528 | tf_op jit(solution)/shard_map/ppermute | solution.py:25
  82.2 7.1 %collective-permute-start.7 = (bf16[1,2,64,640]{3,2,1,0:T(8,128)(2,1)S(1)}, bf16[1,2,64,640]{3,2,1,0:T(8,128)(2,1)S(1)}, u32[]{:S(2)}, u32[]{:S(2)}) collective-permute-start(bf16[1,2,64,640]{3,2,1,0:T(8,128)(2,1)S(1)} %get-tuple-element.58), channel_id=1, source_target_pairs={{0,8},{32,40},{64,72},{96,104},{4,12},{36,44},{68,76},{100,108},{1... | collective-permute-start | bytes 491528 | tf_op jit(solution)/shard_map/ppermute | solution.py:25
  83.5 7.0 %collective-permute-start.8 = (bf16[1,2,64,640]{3,2,1,0:T(8,128)(2,1)S(1)}, bf16[1,2,64,640]{3,2,1,0:T(8,128)(2,1)S(1)}, u32[]{:S(2)}, u32[]{:S(2)}) collective-permute-start(bf16[1,2,64,640]{3,2,1,0:T(8,128)(2,1)S(1)} %get-tuple-element.59), channel_id=1, source_target_pairs={{0,24},{32,56},{64,88},{96,120},{4,28},{36,60},{68,92},{100,124},{... | collective-permute-start | bytes 491528 | tf_op jit(solution)/shard_map/ppermute | solution.py:25
  84.3 8.8 %collective-permute-start.9 = (bf16[1,2,64,640]{3,2,1,0:T(8,128)(2,1)S(1)}, bf16[1,2,64,640]{3,2,1,0:T(8,128)(2,1)S(1)}, u32[]{:S(2)}, u32[]{:S(2)}) collective-permute-start(bf16[1,2,64,640]{3,2,1,0:T(8,128)(2,1)S(1)} %get-tuple-element.60), channel_id=1, source_target_pairs={{0,16},{32,48},{64,80},{96,112},{4,20},{36,52},{68,84},{100,116},{... | collective-permute-start | bytes 491528 | tf_op jit(solution)/shard_map/ppermute | solution.py:25
  94.0 7.2 %collective-permute-start.15 = (bf16[2,64,640]{2,1,0:T(8,128)(2,1)S(1)}, bf16[2,64,640]{2,1,0:T(8,128)(2,1)S(1)}, u32[]{:S(2)}, u32[]{:S(2)}) collective-permute-start(bf16[2,64,640]{2,1,0:T(8,128)(2,1)S(1)} %get-tuple-element.70.p0.refs_8_), channel_id=1, source_target_pairs={{0,8},{32,40},{64,72},{96,104},{4,12},{36,44},{68,76},{100,108},{1... | collective-permute-start | bytes 491528 | tf_op jit(solution)/shard_map/ppermute | solution.py:25
  94.7 8.6 %collective-permute-start.16 = (bf16[2,64,640]{2,1,0:T(8,128)(2,1)S(1)}, bf16[2,64,640]{2,1,0:T(8,128)(2,1)S(1)}, u32[]{:S(2)}, u32[]{:S(2)}) collective-permute-start(bf16[2,64,640]{2,1,0:T(8,128)(2,1)S(1)} %get-tuple-element.70.p0.refs_8_), channel_id=1, source_target_pairs={{0,16},{32,48},{64,80},{96,112},{4,20},{36,52},{68,84},{100,116},{... | collective-permute-start | bytes 491528 | tf_op jit(solution)/shard_map/ppermute | solution.py:25
  98.3 7.2 %collective-permute-start.17 = (bf16[2,64,640]{2,1,0:T(8,128)(2,1)S(1)}, bf16[2,64,640]{2,1,0:T(8,128)(2,1)S(1)}, u32[]{:S(2)}, u32[]{:S(2)}) collective-permute-start(bf16[2,64,640]{2,1,0:T(8,128)(2,1)S(1)} %get-tuple-element.70.p0.refs_8_), channel_id=1, source_target_pairs={{0,24},{32,56},{64,88},{96,120},{4,28},{36,60},{68,92},{100,124},{... | collective-permute-start | bytes 491528 | tf_op jit(solution)/shard_map/ppermute | solution.py:25
  107.2 6.7 %collective-permute-start.18 = (bf16[256,2560]{1,0:T(8,128)(2,1)S(1)}, bf16[256,2560]{1,0:T(8,128)(2,1)S(1)}, u32[]{:S(2)}, u32[]{:S(2)}) collective-permute-start(bf16[256,2560]{1,0:T(8,128)(2,1)S(1)} %shard_map.77), channel_id=1, source_target_pairs={{0,32},{32,0},{64,96},{96,64},{4,36},{36,4},{68,100},{100,68},{1,3... | collective-permute-start | bytes 3932168 | tf_op jit(solution)/shard_map/ppermute | solution.py:25
  109.9 19.2 %collective-permute-start.28 = (bf16[128,2560]{1,0:T(8,128)(2,1)S(1)}, bf16[128,2560]{1,0:T(8,128)(2,1)S(1)}, u32[]{:S(2)}, u32[]{:S(2)}) collective-permute-start(bf16[128,2560]{1,0:T(8,128)(2,1)S(1)} %get-tuple-element.79), channel_id=1, source_target_pairs={{0,4},{32,36},{64,68},{96,100},{4,0},{36,32},{68,64},{100,96},{1,5... | collective-permute-start | bytes 1966088 | tf_op jit(solution)/shard_map/ppermute | solution.py:25
  114.7 17.5 %collective-permute-start.19 = (bf16[2,32,1280]{2,1,0:T(8,128)(2,1)S(1)}, bf16[2,32,1280]{2,1,0:T(8,128)(2,1)S(1)}, u32[]{:S(2)}, u32[]{:S(2)}) collective-permute-start(bf16[2,32,1280]{2,1,0:T(8,128)(2,1)S(1)} %get-tuple-element.72), channel_id=1, source_target_pairs={{0,1},{32,33},{64,65},{96,97},{4,5},{36,37},{68,69},{100,101},{1,2... | collective-permute-start | bytes 491528 | tf_op jit(solution)/shard_map/ppermute | solution.py:25
  115.0 17.7 %collective-permute-start.20 = (bf16[2,32,1280]{2,1,0:T(8,128)(2,1)S(1)}, bf16[2,32,1280]{2,1,0:T(8,128)(2,1)S(1)}, u32[]{:S(2)}, u32[]{:S(2)}) collective-permute-start(bf16[2,32,1280]{2,1,0:T(8,128)(2,1)S(1)} %get-tuple-element.73), channel_id=1, source_target_pairs={{0,3},{32,35},{64,67},{96,99},{4,7},{36,39},{68,71},{100,103},{1,0... | collective-permute-start | bytes 491528 | tf_op jit(solution)/shard_map/ppermute | solution.py:25
  116.8 19.2 %collective-permute-start.21 = (bf16[2,32,1280]{2,1,0:T(8,128)(2,1)S(1)}, bf16[2,32,1280]{2,1,0:T(8,128)(2,1)S(1)}, u32[]{:S(2)}, u32[]{:S(2)}) collective-permute-start(bf16[2,32,1280]{2,1,0:T(8,128)(2,1)S(1)} %get-tuple-element.74), channel_id=1, source_target_pairs={{0,2},{32,34},{64,66},{96,98},{4,6},{36,38},{68,70},{100,102},{1,3... | collective-permute-start | bytes 491528 | tf_op jit(solution)/shard_map/ppermute | solution.py:25
  118.0 27.2 %collective-permute-start.22 = (bf16[128,1280]{1,0:T(8,128)(2,1)S(1)}, bf16[128,1280]{1,0:T(8,128)(2,1)S(1)}, u32[]{:S(2)}, u32[]{:S(2)}) collective-permute-start(bf16[128,1280]{1,0:T(8,128)(2,1)S(1)} %get-tuple-element.75), channel_id=1, source_target_pairs={{0,64},{32,96},{64,4},{96,36},{4,68},{36,100},{68,0},{100,32},{1,6... | collective-permute-start | bytes 983048 | tf_op jit(solution)/shard_map/ppermute | solution.py:25
  129.1 16.2 %collective-permute-start.23 = (bf16[128,1280]{1,0:T(8,128)(2,1)S(1)}, bf16[128,1280]{1,0:T(8,128)(2,1)S(1)}, u32[]{:S(2)}, u32[]{:S(2)}) collective-permute-start(bf16[128,1280]{1,0:T(8,128)(2,1)S(1)} %get-tuple-element.76), channel_id=1, source_target_pairs={{0,68},{32,100},{64,0},{96,32},{4,64},{36,96},{68,4},{100,36},{1,6... | collective-permute-start | bytes 983048 | tf_op jit(solution)/shard_map/ppermute | solution.py:25
  132.2 16.2 %collective-permute-start.34 = (bf16[2,2,64,640]{3,2,1,0:T(8,128)(2,1)S(1)}, bf16[2,2,64,640]{3,2,1,0:T(8,128)(2,1)S(1)}, u32[]{:S(2)}, u32[]{:S(2)}) collective-permute-start(bf16[2,2,64,640]{3,2,1,0:T(8,128)(2,1)S(1)} %get-tuple-element.86.refs_4_), channel_id=1, source_target_pairs={{0,8},{32,40},{64,72},{96,104},{4,12},{36,44},{68,76},{100,108},{1... | collective-permute-start | bytes 983048 | tf_op jit(solution)/shard_map/ppermute | solution.py:25
  132.8 16.9 %collective-permute-start.35 = (bf16[2,2,64,640]{3,2,1,0:T(8,128)(2,1)S(1)}, bf16[2,2,64,640]{3,2,1,0:T(8,128)(2,1)S(1)}, u32[]{:S(2)}, u32[]{:S(2)}) collective-permute-start(bf16[2,2,64,640]{3,2,1,0:T(8,128)(2,1)S(1)} %get-tuple-element.86.refs_4_), channel_id=1, source_target_pairs={{0,16},{32,48},{64,80},{96,112},{4,20},{36,52},{68,84},{100,116},{... | collective-permute-start | bytes 983048 | tf_op jit(solution)/shard_map/ppermute | solution.py:25
  136.0 14.0 %collective-permute-start.36 = (bf16[2,2,64,640]{3,2,1,0:T(8,128)(2,1)S(1)}, bf16[2,2,64,640]{3,2,1,0:T(8,128)(2,1)S(1)}, u32[]{:S(2)}, u32[]{:S(2)}) collective-permute-start(bf16[2,2,64,640]{3,2,1,0:T(8,128)(2,1)S(1)} %get-tuple-element.86.refs_4_), channel_id=1, source_target_pairs={{0,24},{32,56},{64,88},{96,120},{4,28},{36,60},{68,92},{100,124},{... | collective-permute-start | bytes 983048 | tf_op jit(solution)/shard_map/ppermute | solution.py:25
  146.1 13.7 %collective-permute-start.29 = (bf16[32,2560]{1,0:T(8,128)(2,1)S(1)}, bf16[32,2560]{1,0:T(8,128)(2,1)S(1)}, u32[]{:S(2)}, u32[]{:S(2)}) collective-permute-start(bf16[32,2560]{1,0:T(8,128)(2,1)S(1)} %get-tuple-element.81), channel_id=1, source_target_pairs={{0,1},{32,33},{64,65},{96,97},{4,5},{36,37},{68,69},{100,101},{1,2... | collective-permute-start | bytes 491528 | tf_op jit(solution)/shard_map/ppermute | solution.py:25
  146.6 13.2 %collective-permute-start.30 = (bf16[32,2560]{1,0:T(8,128)(2,1)S(1)}, bf16[32,2560]{1,0:T(8,128)(2,1)S(1)}, u32[]{:S(2)}, u32[]{:S(2)}) collective-permute-start(bf16[32,2560]{1,0:T(8,128)(2,1)S(1)} %get-tuple-element.82), channel_id=1, source_target_pairs={{0,3},{32,35},{64,67},{96,99},{4,7},{36,39},{68,71},{100,103},{1,0... | collective-permute-start | bytes 491528 | tf_op jit(solution)/shard_map/ppermute | solution.py:25
  148.4 11.4 %collective-permute-start.31 = (bf16[32,2560]{1,0:T(8,128)(2,1)S(1)}, bf16[32,2560]{1,0:T(8,128)(2,1)S(1)}, u32[]{:S(2)}, u32[]{:S(2)}) collective-permute-start(bf16[32,2560]{1,0:T(8,128)(2,1)S(1)} %get-tuple-element.83), channel_id=1, source_target_pairs={{0,2},{32,34},{64,66},{96,98},{4,6},{36,38},{68,70},{100,102},{1,3... | collective-permute-start | bytes 491528 | tf_op jit(solution)/shard_map/ppermute | solution.py:25
  149.7 10.1 %collective-permute-start.32 = (bf16[32,1280]{1,0:T(8,128)(2,1)S(1)}, bf16[32,1280]{1,0:T(8,128)(2,1)S(1)}, u32[]{:S(2)}, u32[]{:S(2)}) collective-permute-start(bf16[32,1280]{1,0:T(8,128)(2,1)S(1)} %get-tuple-element.84), channel_id=1, source_target_pairs={{0,64},{32,96},{64,4},{96,36},{4,68},{36,100},{68,0},{100,32},{1,6... | collective-permute-start | bytes 245768 | tf_op jit(solution)/shard_map/ppermute | solution.py:25
  150.0 9.7 %collective-permute-start.33 = (bf16[32,1280]{1,0:T(8,128)(2,1)S(1)}, bf16[32,1280]{1,0:T(8,128)(2,1)S(1)}, u32[]{:S(2)}, u32[]{:S(2)}) collective-permute-start(bf16[32,1280]{1,0:T(8,128)(2,1)S(1)} %get-tuple-element.85), channel_id=1, source_target_pairs={{0,68},{32,100},{64,0},{96,32},{4,64},{36,96},{68,4},{100,36},{1,6... | collective-permute-start | bytes 245768 | tf_op jit(solution)/shard_map/ppermute | solution.py:25
